TPU v7x, 128 devices: a whole 4x4x4 slice. The times are simulated.
128 devices in a mesh: wide: 16 (over y_lo, z, core), narrow: 8 (over x, y_hi).
Axes of the slice: x: 4, y: 4 (y_hi: 2, y_lo: 2; y = y_hi * 2 + y_lo), z: 4, core: 2. Of those that a mesh axis runs over, the one named last changes fastest.
Arguments:
- fields: float32 [5, 16, 64, 256], P(None, 'wide', 'narrow'), may hold values from -2.1 to 6.1, as said below
- prior_modes: bfloat16 [124, 5, 16, 16384], P(None, None, 'wide', 'narrow'), may hold values from -360 to 360, as said below
Outputs:
- flow_state: float32 [5, 16, 64, 256], P(None, 'wide', 'narrow')
- factor: float32 [128, 128], replicated
Inputs may be any that keep to these rules, and one draw needn't show every extreme that they name: `fields`: density and pressure lie in 0.6 to 1.4, each velocity component below 1.5 in magnitude. `prior_modes`: the columns are linearly independent.
All inputs are finite; a program needn't handle non-finite values.
Results may differ from a plain program's by a relative error of at most 0.0014.
Values may be sent and summed in bfloat16 or wider, within the bound.
No kernel may reach another device: no remote copies, remote signals or barrier semaphores. Data moves between devices by JAX's collectives and lax.ppermute only.
A program may use at most 64 MiB of HBM per device.

v0:
```python
import jax
import jax.numpy as jnp
from jax import lax
from jax.sharding import PartitionSpec as P

STEPS = 2


GAMMA = 1.4
TIME_STEP = 0.25
VISCOSITY = 0.15


def extended(block, sides, width):
    for axis, dim in sides:
        count = lax.axis_size(axis)
        forward = [(i, i + 1) for i in range(count - 1)]
        forward.append((count - 1, 0))
        backward = [(target, source) for source, target in forward]
        low = lax.ppermute(
            lax.slice_in_dim(block, block.shape[dim] - width, None, axis=dim), axis, forward
        )
        high = lax.ppermute(lax.slice_in_dim(block, 0, width, axis=dim), axis, backward)
        block = jnp.concatenate([low, block, high], axis=dim)
    return block


def flux_of(current, dim_index):
    density = current[0]
    momentum = current[1:4]
    energy = current[4]
    vel_d = momentum[dim_index] / density
    pressure = (GAMMA - 1.0) * (
        energy
        - 0.5
        * (momentum[0] * momentum[0] + momentum[1] * momentum[1] + momentum[2] * momentum[2])
        / density
    )
    components = [
        momentum[dim_index],
        momentum[0] * vel_d,
        momentum[1] * vel_d,
        momentum[2] * vel_d,
        (energy + pressure) * vel_d,
    ]
    components[1 + dim_index] = components[1 + dim_index] + pressure
    return jnp.stack(components)


def tendency(current):
    padded = extended(current.astype(jnp.bfloat16), (("wide", 1), ("narrow", 2)), 1).astype(
        current.dtype
    )
    flux_x = flux_of(padded[:, :, 1:-1], 0)
    flux_y = flux_of(padded[:, 1:-1, :], 1)
    flux_z = flux_of(current, 2)
    divergence = (
        flux_x[:, 2:]
        - flux_x[:, :-2]
        + (flux_y[:, :, 2:] - flux_y[:, :, :-2])
        + (jnp.roll(flux_z, -1, 3) - jnp.roll(flux_z, 1, 3))
    )
    laplace = (
        padded[:, 2:, 1:-1]
        + padded[:, :-2, 1:-1]
        + padded[:, 1:-1, 2:]
        + padded[:, 1:-1, :-2]
        + jnp.roll(current, -1, 3)
        + jnp.roll(current, 1, 3)
        - 6.0 * current
    )
    return -0.5 * divergence + VISCOSITY * laplace


def local(fields, prior_modes):
    wide_count = lax.axis_size("wide")
    narrow_count = lax.axis_size("narrow")
    cells_x, cells_y, cells_z = (fields.shape[1], fields.shape[2], fields.shape[3])
    inverse_cells = 1.0 / (cells_x * wide_count * cells_y * narrow_count * cells_z)
    flat_modes = prior_modes.reshape(prior_modes.shape[0], -1)
    contract = (((1,), (1,)), ((), ()))
    gram_modes = lax.dot_general(
        flat_modes, flat_modes, contract, preferred_element_type=jnp.float32
    )
    current = fields
    snapshots = []
    for step_index in range(STEPS):
        section_one = current + TIME_STEP * tendency(current)
        snapshots.append(section_one.astype(jnp.bfloat16))
        current = 0.5 * current + 0.5 * (section_one + TIME_STEP * tendency(section_one))
        snapshots.append(current.astype(jnp.bfloat16))
    arrived = lax.all_to_all(
        jnp.stack(snapshots), "narrow", split_axis=4, concat_axis=3, tiled=True
    )
    snap_rows = jnp.swapaxes(arrived, 3, 4).reshape(arrived.shape[0], -1)
    cross_gram = lax.dot_general(
        flat_modes, snap_rows, contract, preferred_element_type=jnp.float32
    )
    snap_gram = lax.dot_general(snap_rows, snap_rows, contract, preferred_element_type=jnp.float32)
    gram_local = jnp.concatenate(
        [
            jnp.concatenate([gram_modes, cross_gram], 1),
            jnp.concatenate([cross_gram.T, snap_gram], 1),
        ],
        0,
    )
    gram_local = gram_local * inverse_cells
    gram_whole = lax.psum(gram_local, ("wide", "narrow"))
    factor = jnp.linalg.cholesky(gram_whole).T
    return (current, factor)


def solution(mesh):
    placed = (P(None, "wide", "narrow", None), P(None, None, "wide", "narrow"))
    return jax.shard_map(
        local,
        mesh=mesh,
        in_specs=placed,
        out_specs=(P(None, "wide", "narrow", None), P()),
        check_vma=False,
    )
```

profile of v0, /device:TPU:0, one launch (start us, length us, event | category | flops | bytes accessed | tf_op | source)
XLA Modules:
  0.0 252.9 jit_solution(13830206497082720852)
XLA Ops:
  7.9 4.6 %collective-permute-start.1 = (bf16[5,1,8,256]{3,2,1,0:T(8,128)(2,1)S(1)}, bf16[5,1,8,256]{3,2,1,0:T(8,128)(2,1)S(1)}, u32[]{:S(2)}, u32[]{:S(2)}) collective-permute-start(bf16[5,1,8,256]{3,2,1,0:T(8,128)(2,1)S(1)} %convert_element_type.30), channel_id=1, source_target_pairs={{8,0},{16,8},{24,16},{32,24},{40,32},{48,40},{56,48},{64,56},{72,6... | collective-permute-start | bytes 61448 | tf_op jit(solution)/shard_map/ppermute | solution.py:23
  16.2 0.9 fusion.98
  17.9 5.2 %collective-permute-start.3 = (bf16[5,3,1,256]{3,1,2,0:T(4,128)(2,1)S(1)}, bf16[5,3,1,256]{3,1,2,0:T(4,128)(2,1)S(1)}, u32[]{:S(2)}, u32[]{:S(2)}) collective-permute-start(bf16[5,3,1,256]{3,1,2,0:T(4,128)(2,1)S(1)} %copy.427), channel_id=1, source_target_pairs={{1,0},{2,1},{3,2},{4,3},{5,4},{6,5},{7,6},{0,7},{9,8},{10,9},{11,1... | collective-permute-start | bytes 23048 | tf_op jit(solution)/shard_map/ppermute | solution.py:23
  23.1 0.8 fusion.99
  24.5 5.9 %collective-permute-done.2 = bf16[5,3,1,256]{3,1,2,0:T(4,128)(2,1)S(1)} collective-permute-done((bf16[5,3,1,256]{3,1,2,0:T(4,128)(2,1)S(1)}, bf16[5,3,1,256]{3,1,2,0:T(4,128)(2,1)S(1)}, u32[]{:S(2)}, u32[]{:S(2)}) %collective-permute-start.2) | collective-permute-done | bytes 7712 | tf_op jit(solution)/shard_map/ppermute | solution.py:20
  30.7 0.9 fusion.83
  31.6 1.2 collective-permute-start.5
  33.1 1.2 collective-permute-done.5
  34.3 3.8 %collective-permute-done.4 = bf16[5,1,8,256]{3,2,0,1:T(8,128)(2,1)S(1)} collective-permute-done((bf16[5,1,8,256]{3,2,0,1:T(8,128)(2,1)S(1)}, bf16[5,1,8,256]{3,2,0,1:T(8,128)(2,1)S(1)}, u32[]{:S(2)}, u32[]{:S(2)}) %collective-permute-start.4) | collective-permute-done | bytes 20512 | tf_op jit(solution)/shard_map/ppermute | solution.py:20
  38.2 1.0 collective-permute-start.7
  39.1 2.6 %collective-permute-start.6 = (bf16[5,3,1,256]{3,1,2,0:T(4,128)(2,1)S(1)}, bf16[5,3,1,256]{3,1,2,0:T(4,128)(2,1)S(1)}, u32[]{:S(2)}, u32[]{:S(2)}) collective-permute-start(bf16[5,3,1,256]{3,1,2,0:T(4,128)(2,1)S(1)} %copy.382), channel_id=1, source_target_pairs={{0,1},{1,2},{2,3},{3,4},{4,5},{5,6},{6,7},{7,0},{8,9},{9,10},{10,1... | collective-permute-start | bytes 23048 | tf_op jit(solution)/shard_map/ppermute | solution.py:20
  41.8 1.6 collective-permute-done.7
  43.4 3.0 %collective-permute-done.6 = bf16[5,3,1,256]{3,1,2,0:T(4,128)(2,1)S(1)} collective-permute-done((bf16[5,3,1,256]{3,1,2,0:T(4,128)(2,1)S(1)}, bf16[5,3,1,256]{3,1,2,0:T(4,128)(2,1)S(1)}, u32[]{:S(2)}, u32[]{:S(2)}) %collective-permute-start.6) | collective-permute-done | bytes 7712 | tf_op jit(solution)/shard_map/ppermute | solution.py:20
  48.6 3.9 %collective-permute-done.8 = bf16[5,1,8,256]{3,2,0,1:T(8,128)(2,1)S(1)} collective-permute-done((bf16[5,1,8,256]{3,2,0,1:T(8,128)(2,1)S(1)}, bf16[5,1,8,256]{3,2,0,1:T(8,128)(2,1)S(1)}, u32[]{:S(2)}, u32[]{:S(2)}) %collective-permute-start.8) | collective-permute-done | bytes 20512 | tf_op jit(solution)/shard_map/ppermute | solution.py:20
  52.6 3.5 %collective-permute-start.10 = (bf16[5,3,1,256]{3,1,2,0:T(4,128)(2,1)S(1)}, bf16[5,3,1,256]{3,1,2,0:T(4,128)(2,1)S(1)}, u32[]{:S(2)}, u32[]{:S(2)}) collective-permute-start(bf16[5,3,1,256]{3,1,2,0:T(4,128)(2,1)S(1)} %copy.394), channel_id=1, source_target_pairs={{0,1},{1,2},{2,3},{3,4},{4,5},{5,6},{6,7},{7,0},{8,9},{9,10},{10,1... | collective-permute-start | bytes 23048 | tf_op jit(solution)/shard_map/ppermute | solution.py:20
  56.1 1.6 collective-permute-done.11
  57.8 2.2 collective-permute-done.10
  62.0 4.0 %collective-permute-done.12 = bf16[5,1,8,256]{3,2,0,1:T(8,128)(2,1)S(1)} collective-permute-done((bf16[5,1,8,256]{3,2,0,1:T(8,128)(2,1)S(1)}, bf16[5,1,8,256]{3,2,0,1:T(8,128)(2,1)S(1)}, u32[]{:S(2)}, u32[]{:S(2)}) %collective-permute-start.12) | collective-permute-done | bytes 20512 | tf_op jit(solution)/shard_map/ppermute | solution.py:20
  66.1 3.5 %collective-permute-start.14 = (bf16[5,3,1,256]{3,1,2,0:T(4,128)(2,1)S(1)}, bf16[5,3,1,256]{3,1,2,0:T(4,128)(2,1)S(1)}, u32[]{:S(2)}, u32[]{:S(2)}) collective-permute-start(bf16[5,3,1,256]{3,1,2,0:T(4,128)(2,1)S(1)} %copy.405), channel_id=1, source_target_pairs={{0,1},{1,2},{2,3},{3,4},{4,5},{5,6},{6,7},{7,0},{8,9},{9,10},{10,1... | collective-permute-start | bytes 23048 | tf_op jit(solution)/shard_map/ppermute | solution.py:20
  69.7 1.6 collective-permute-done.15
  71.3 2.2 collective-permute-done.14
  75.3 2.1 reshape.630
  77.4 3.4 %all-to-all-start = ((bf16[8,2,2560]{2,1,0:T(2,128)(2,1)}), bf16[8,2,2560]{2,1,0:T(2,128)(2,1)S(1)}, u32[]{:S(2)}, u32[]{:S(2)}) async-start(bf16[8,2,2560]{2,1,0:T(2,128)(2,1)} %reshape.630), calls=%async_computation | async-start | bytes 163840 | tf_op jit(solution)/shard_map/all_to_all | solution.py:92
  80.9 3.4 %fusion.2 = f32[124,124]{0,1:T(8,128)S(1)} fusion(bf16[124,5,1,2048]{3,0,2,1:T(8,128)(2,1)} %param.3), kind=kOutput, calls=%fused_computation.2 | convolution fusion | flops 314900480 | bytes 2601024 | tf_op jit(solution)/shard_map/dot_general | solution.py:82
  84.3 3.3 %copy.420 = bf16[124,5,1,2048]{0,3,1,2:T(8,128)(2,1)S(1)} copy(bf16[124,5,1,2048]{3,0,2,1:T(8,128)(2,1)} %param.3) | data formatting | bytes 5079040 | tf_op args[1]
  87.6 0.8 all-to-all-done
  88.4 2.6 %reshape.631 = bf16[256,5,1,4,8]{4,3,2,1,0:T(4,128)(2,1)} reshape(bf16[8,2,2560]{2,1,0:T(2,128)(2,1)S(1)} %all-to-all-done) | data formatting | bytes 163840
  91.0 1.8 copy.417
  94.9 135.5 %all-reduce.2.cloned.1.call-done = f32[128,128]{0,1:T(8,128)} async-done(((f32[128,128]{0,1:T(8,128)}), f32[128,128]{0,1:T(8,128)}) %all-reduce.2.cloned.1.call-update) | async-done | bytes 65552 | tf_op jit(solution)/shard_map/psum | solution.py:108
  230.4 0.9 copy.422
  231.4 0.9 fusion.6
  232.2 11.7 %cholesky.18 = f32[128,128]{1,0:T(8,128)S(1)} custom-call(f32[128,128]{1,0:T(8,128)S(1)} %fusion.6), custom_call_target="Cholesky" | custom-call | tf_op jit(solution)/shard_map/jit(cholesky)/cholesky | solution.py:109
  (135 shorter events, 16.7 us)
Async XLA Ops:
  7.9 9.2 %collective-permute-start.1 = (bf16[5,1,8,256]{3,2,1,0:T(8,128)(2,1)S(1)}, bf16[5,1,8,256]{3,2,1,0:T(8,128)(2,1)S(1)}, u32[]{:S(2)}, u32[]{:S(2)}) collective-permute-start(bf16[5,1,8,256]{3,2,1,0:T(8,128)(2,1)S(1)} %convert_element_type.30), channel_id=1, source_target_pairs={{8,0},{16,8},{24,16},{32,24},{40,32},{48,40},{56,48},{64,56},{72,6... | collective-permute-start | bytes 61448 | tf_op jit(solution)/shard_map/ppermute | solution.py:23
  12.5 5.3 %collective-permute-start = (bf16[5,1,8,256]{3,2,1,0:T(8,128)(2,1)S(1)}, bf16[5,1,8,256]{3,2,1,0:T(8,128)(2,1)S(1)}, u32[]{:S(2)}, u32[]{:S(2)}) collective-permute-start(bf16[5,1,8,256]{3,2,1,0:T(8,128)(2,1)S(1)} %convert_element_type.30), channel_id=1, source_target_pairs={{0,8},{8,16},{16,24},{24,32},{32,40},{40,48},{48,56},{56,64},{64,7... | collective-permute-start | bytes 61448 | tf_op jit(solution)/shard_map/ppermute | solution.py:20
  13.3 33.5 %copy-start = (f32[5,1,8,256]{3,2,1,0:T(8,128)S(1)}, f32[5,1,8,256]{3,2,1,0:T(8,128)}, u32[]{:S(2)}) copy-start(f32[5,1,8,256]{3,2,1,0:T(8,128)} %param.2) | copy-start | bytes 122884
  17.9 6.5 %collective-permute-start.3 = (bf16[5,3,1,256]{3,1,2,0:T(4,128)(2,1)S(1)}, bf16[5,3,1,256]{3,1,2,0:T(4,128)(2,1)S(1)}, u32[]{:S(2)}, u32[]{:S(2)}) collective-permute-start(bf16[5,3,1,256]{3,1,2,0:T(4,128)(2,1)S(1)} %copy.427), channel_id=1, source_target_pairs={{1,0},{2,1},{3,2},{4,3},{5,4},{6,5},{7,6},{0,7},{9,8},{10,9},{11,1... | collective-permute-start | bytes 23048 | tf_op jit(solution)/shard_map/ppermute | solution.py:23
  23.1 7.3 %collective-permute-start.2 = (bf16[5,3,1,256]{3,1,2,0:T(4,128)(2,1)S(1)}, bf16[5,3,1,256]{3,1,2,0:T(4,128)(2,1)S(1)}, u32[]{:S(2)}, u32[]{:S(2)}) collective-permute-start(bf16[5,3,1,256]{3,1,2,0:T(4,128)(2,1)S(1)} %copy.426), channel_id=1, source_target_pairs={{0,1},{1,2},{2,3},{3,4},{4,5},{5,6},{6,7},{7,0},{8,9},{9,10},{10,1... | collective-permute-start | bytes 23048 | tf_op jit(solution)/shard_map/ppermute | solution.py:20
  31.6 2.7 %collective-permute-start.5 = (bf16[5,1,8,256]{3,2,0,1:T(8,128)(2,1)S(1)}, bf16[5,1,8,256]{3,2,0,1:T(8,128)(2,1)S(1)}, u32[]{:S(2)}, u32[]{:S(2)}) collective-permute-start(bf16[5,1,8,256]{3,2,0,1:T(8,128)(2,1)S(1)} %get-tuple-element.65), channel_id=1, source_target_pairs={{8,0},{16,8},{24,16},{32,24},{40,32},{48,40},{56,48},{64,56},{72,6... | collective-permute-start | bytes 61448 | tf_op jit(solution)/shard_map/ppermute | solution.py:23
  32.8 5.3 %collective-permute-start.4 = (bf16[5,1,8,256]{3,2,0,1:T(8,128)(2,1)S(1)}, bf16[5,1,8,256]{3,2,0,1:T(8,128)(2,1)S(1)}, u32[]{:S(2)}, u32[]{:S(2)}) collective-permute-start(bf16[5,1,8,256]{3,2,0,1:T(8,128)(2,1)S(1)} %get-tuple-element.65), channel_id=1, source_target_pairs={{0,8},{8,16},{16,24},{24,32},{32,40},{40,48},{48,56},{56,64},{64,7... | collective-permute-start | bytes 61448 | tf_op jit(solution)/shard_map/ppermute | solution.py:20
  38.2 5.2 %collective-permute-start.7 = (bf16[5,3,1,256]{3,1,2,0:T(4,128)(2,1)S(1)}, bf16[5,3,1,256]{3,1,2,0:T(4,128)(2,1)S(1)}, u32[]{:S(2)}, u32[]{:S(2)}) collective-permute-start(bf16[5,3,1,256]{3,1,2,0:T(4,128)(2,1)S(1)} %copy.383), channel_id=1, source_target_pairs={{1,0},{2,1},{3,2},{4,3},{5,4},{6,5},{7,6},{0,7},{9,8},{10,9},{11,1... | collective-permute-start | bytes 23048 | tf_op jit(solution)/shard_map/ppermute | solution.py:23
  39.1 7.3 %collective-permute-start.6 = (bf16[5,3,1,256]{3,1,2,0:T(4,128)(2,1)S(1)}, bf16[5,3,1,256]{3,1,2,0:T(4,128)(2,1)S(1)}, u32[]{:S(2)}, u32[]{:S(2)}) collective-permute-start(bf16[5,3,1,256]{3,1,2,0:T(4,128)(2,1)S(1)} %copy.382), channel_id=1, source_target_pairs={{0,1},{1,2},{2,3},{3,4},{4,5},{5,6},{6,7},{7,0},{8,9},{9,10},{10,1... | collective-permute-start | bytes 23048 | tf_op jit(solution)/shard_map/ppermute | solution.py:20
  47.0 1.5 collective-permute-start.9
  47.1 5.4 %collective-permute-start.8 = (bf16[5,1,8,256]{3,2,0,1:T(8,128)(2,1)S(1)}, bf16[5,1,8,256]{3,2,0,1:T(8,128)(2,1)S(1)}, u32[]{:S(2)}, u32[]{:S(2)}) collective-permute-start(bf16[5,1,8,256]{3,2,0,1:T(8,128)(2,1)S(1)} %fusion.78), channel_id=1, source_target_pairs={{0,8},{8,16},{16,24},{24,32},{32,40},{40,48},{48,56},{56,64},{64,7... | collective-permute-start | bytes 61448 | tf_op jit(solution)/shard_map/ppermute | solution.py:20
  52.5 5.2 %collective-permute-start.11 = (bf16[5,3,1,256]{3,1,2,0:T(4,128)(2,1)S(1)}, bf16[5,3,1,256]{3,1,2,0:T(4,128)(2,1)S(1)}, u32[]{:S(2)}, u32[]{:S(2)}) collective-permute-start(bf16[5,3,1,256]{3,1,2,0:T(4,128)(2,1)S(1)} %copy.395), channel_id=1, source_target_pairs={{1,0},{2,1},{3,2},{4,3},{5,4},{6,5},{7,6},{0,7},{9,8},{10,9},{11,1... | collective-permute-start | bytes 23048 | tf_op jit(solution)/shard_map/ppermute | solution.py:23
  52.6 7.4 %collective-permute-start.10 = (bf16[5,3,1,256]{3,1,2,0:T(4,128)(2,1)S(1)}, bf16[5,3,1,256]{3,1,2,0:T(4,128)(2,1)S(1)}, u32[]{:S(2)}, u32[]{:S(2)}) collective-permute-start(bf16[5,3,1,256]{3,1,2,0:T(4,128)(2,1)S(1)} %copy.394), channel_id=1, source_target_pairs={{0,1},{1,2},{2,3},{3,4},{4,5},{5,6},{6,7},{7,0},{8,9},{9,10},{10,1... | collective-permute-start | bytes 23048 | tf_op jit(solution)/shard_map/ppermute | solution.py:20
  60.4 1.6 collective-permute-start.13
  60.5 5.5 %collective-permute-start.12 = (bf16[5,1,8,256]{3,2,0,1:T(8,128)(2,1)S(1)}, bf16[5,1,8,256]{3,2,0,1:T(8,128)(2,1)S(1)}, u32[]{:S(2)}, u32[]{:S(2)}) collective-permute-start(bf16[5,1,8,256]{3,2,0,1:T(8,128)(2,1)S(1)} %get-tuple-element.31), channel_id=1, source_target_pairs={{0,8},{8,16},{16,24},{24,32},{32,40},{40,48},{48,56},{56,64},{64,7... | collective-permute-start | bytes 61448 | tf_op jit(solution)/shard_map/ppermute | solution.py:20
  66.0 5.2 %collective-permute-start.15 = (bf16[5,3,1,256]{3,1,2,0:T(4,128)(2,1)S(1)}, bf16[5,3,1,256]{3,1,2,0:T(4,128)(2,1)S(1)}, u32[]{:S(2)}, u32[]{:S(2)}) collective-permute-start(bf16[5,3,1,256]{3,1,2,0:T(4,128)(2,1)S(1)} %copy.406), channel_id=1, source_target_pairs={{1,0},{2,1},{3,2},{4,3},{5,4},{6,5},{7,6},{0,7},{9,8},{10,9},{11,1... | collective-permute-start | bytes 23048 | tf_op jit(solution)/shard_map/ppermute | solution.py:23
  66.1 7.4 %collective-permute-start.14 = (bf16[5,3,1,256]{3,1,2,0:T(4,128)(2,1)S(1)}, bf16[5,3,1,256]{3,1,2,0:T(4,128)(2,1)S(1)}, u32[]{:S(2)}, u32[]{:S(2)}) collective-permute-start(bf16[5,3,1,256]{3,1,2,0:T(4,128)(2,1)S(1)} %copy.405), channel_id=1, source_target_pairs={{0,1},{1,2},{2,3},{3,4},{4,5},{5,6},{6,7},{7,0},{8,9},{9,10},{10,1... | collective-permute-start | bytes 23048 | tf_op jit(solution)/shard_map/ppermute | solution.py:20
  77.4 11.1 %all-to-all-start = ((bf16[8,2,2560]{2,1,0:T(2,128)(2,1)}), bf16[8,2,2560]{2,1,0:T(2,128)(2,1)S(1)}, u32[]{:S(2)}, u32[]{:S(2)}) async-start(bf16[8,2,2560]{2,1,0:T(2,128)(2,1)} %reshape.630), calls=%async_computation | async-start | bytes 163840 | tf_op jit(solution)/shard_map/all_to_all | solution.py:92
  80.7 149.7 %all-reduce.2.cloned.1.call-start = ((), (), s32[]{:S(2)}) async-start(), calls=%async_computation.1 | async-start | bytes 131072 | tf_op jit(solution)/shard_map/psum | solution.py:108
Sparse Core Ops, SparseCore 0:
  95.1 135.3 all-reduce.1
where the time goes:
time: 257 us; the launch traced here: 253 us
  waiting for transfers between devices  170 us (66%)
  starting transfers between devices  26.5 us (10%)
  other arithmetic  21.4 us (8%)
  local copies, waits for them, and re-layouts  16.3 us (6%)
  between operations  14.6 us (6%)
  matrix products  4.11 us (2%)
    psum x1, waiting for transfers between devices, local(): gram_whole = lax.psum(gram_local, ('wide', 'narrow'))  135 us
    ppermute x8, waiting for transfers between devices, extended(): lax.ppermute(lax.slice_in_dim(block, block.shape[dim] - width, None, axis...  25.7 us
    another operation x3, other arithmetic, local(): factor = jnp.linalg.cholesky(gram_whole).T  12.4 us
    ppermute x8, starting transfers between devices, extended(): lax.ppermute(lax.slice_in_dim(block, 0, width, axis=dim), axis, backward)  12.2 us
    ppermute x8, starting transfers between devices, extended(): lax.ppermute(lax.slice_in_dim(block, block.shape[dim] - width, None, axis...  10.6 us
    unnamed x16, local copies, waits for them, and re-layouts  9.47 us
    ppermute x8, waiting for transfers between devices, extended(): lax.ppermute(lax.slice_in_dim(block, 0, width, axis=dim), axis, backward)  7.97 us
  transfers between devices with their start and end apart: 18, of which 17 were waited for; matrix products, arithmetic and copies ran while one was open for 5% of the time, Pallas kernels for 0%

commit v1 on v0

--- a/solution.py
+++ b/solution.py
@@ -105,7 +105,14 @@
         0,
     )
     gram_local = gram_local * inverse_cells
-    gram_whole = lax.psum(gram_local, ("wide", "narrow"))
+    devices = wide_count * narrow_count
+    everywhere = ("wide", "narrow")
+    pieces = gram_local.reshape(devices, 1, -1)
+    pieces = lax.all_to_all(pieces, everywhere, split_axis=0, concat_axis=0, tiled=True)
+    piece = jnp.sum(pieces, axis=0, keepdims=True)
+    copies = jnp.broadcast_to(piece, pieces.shape)
+    copies = lax.all_to_all(copies, everywhere, split_axis=0, concat_axis=0, tiled=True)
+    gram_whole = copies.reshape(gram_local.shape)
     factor = jnp.linalg.cholesky(gram_whole).T
     return (current, factor)
 

time: 257 us -> 133 us (0.52); the launches traced: 253 us -> 132 us
  waiting for transfers between devices: 170 us -> 34.6 us
  blocking collectives: 0 us -> 29.8 us
  between operations: 14.6 us -> 1.28 us
    psum x1 -> x0, waiting for transfers between devices: 135 us -> none  [local(): gram_whole = lax.psum(gram_local, ('wide', 'narrow'))]
    all_to_all x0 -> x2, blocking collectives: none -> 29.8 us  [the longest x1 16 us: local(): lax.all_to_all(pieces, everywhere, split_axis=0, concat_axis=0, tiled=True)]
  transfers between devices with their start and end apart: 18 -> 17, of which waited for: 17 -> 16; matrix products, arithmetic and copies ran while one was open for 5% -> 10% of each run, Pallas kernels for 0% -> 0%
where the time goes in v1:
time: 133 us; the launch traced here: 132 us
  waiting for transfers between devices  34.6 us (26%)
  blocking collectives  29.8 us (22%)
  starting transfers between devices  26.4 us (20%)
  other arithmetic  20.1 us (15%)
  local copies, waits for them, and re-layouts  15.5 us (12%)
  matrix products  4.09 us (3%)
    ppermute x8, waiting for transfers between devices, extended(): lax.ppermute(lax.slice_in_dim(block, block.shape[dim] - width, None, axis...  25.7 us
    all_to_all x1, blocking collectives, local(): lax.all_to_all(pieces, everywhere, split_axis=0, concat_axis=0, tiled=True)  16 us
    all_to_all x1, blocking collectives, local(): lax.all_to_all(copies, everywhere, split_axis=0, concat_axis=0, tiled=True)  13.8 us
    another operation x3, other arithmetic, local(): factor = jnp.linalg.cholesky(gram_whole).T  12.4 us
    ppermute x8, starting transfers between devices, extended(): lax.ppermute(lax.slice_in_dim(block, 0, width, axis=dim), axis, backward)  12.2 us
    ppermute x8, starting transfers between devices, extended(): lax.ppermute(lax.slice_in_dim(block, block.shape[dim] - width, None, axis...  10.6 us
    unnamed x16, local copies, waits for them, and re-layouts  9.42 us
    ppermute x8, waiting for transfers between devices, extended(): lax.ppermute(lax.slice_in_dim(block, 0, width, axis=dim), axis, backward)  7.97 us
  transfers between devices with their start and end apart: 17, of which 16 were waited for; matrix products, arithmetic and copies ran while one was open for 10% of the time, Pallas kernels for 0%

profile of v1, /device:TPU:0, one launch (start us, length us, event | category | flops | bytes accessed | tf_op | source)
XLA Modules:
  0.0 131.7 jit_solution(1061865496528465805)
XLA Ops:
  0.6 0.8 convert_element_type.30
  1.4 4.6 %collective-permute-start.1 = (bf16[5,1,8,256]{3,2,1,0:T(8,128)(2,1)S(1)}, bf16[5,1,8,256]{3,2,1,0:T(8,128)(2,1)S(1)}, u32[]{:S(2)}, u32[]{:S(2)}) collective-permute-start(bf16[5,1,8,256]{3,2,1,0:T(8,128)(2,1)S(1)} %convert_element_type.30), channel_id=1, source_target_pairs={{8,0},{16,8},{24,16},{32,24},{40,32},{48,40},{56,48},{64,56},{72,6... | collective-permute-start | bytes 61448 | tf_op jit(solution)/shard_map/ppermute | solution.py:23
  9.7 0.9 fusion.98
  11.4 5.2 %collective-permute-start.3 = (bf16[5,3,1,256]{3,1,2,0:T(4,128)(2,1)S(1)}, bf16[5,3,1,256]{3,1,2,0:T(4,128)(2,1)S(1)}, u32[]{:S(2)}, u32[]{:S(2)}) collective-permute-start(bf16[5,3,1,256]{3,1,2,0:T(4,128)(2,1)S(1)} %copy.436), channel_id=1, source_target_pairs={{1,0},{2,1},{3,2},{4,3},{5,4},{6,5},{7,6},{0,7},{9,8},{10,9},{11,1... | collective-permute-start | bytes 23048 | tf_op jit(solution)/shard_map/ppermute | solution.py:23
  16.6 0.8 fusion.99
  18.0 5.9 %collective-permute-done.2 = bf16[5,3,1,256]{3,1,2,0:T(4,128)(2,1)S(1)} collective-permute-done((bf16[5,3,1,256]{3,1,2,0:T(4,128)(2,1)S(1)}, bf16[5,3,1,256]{3,1,2,0:T(4,128)(2,1)S(1)}, u32[]{:S(2)}, u32[]{:S(2)}) %collective-permute-start.2) | collective-permute-done | bytes 7712 | tf_op jit(solution)/shard_map/ppermute | solution.py:20
  24.2 0.9 fusion.83
  25.1 1.2 collective-permute-start.5
  26.5 1.2 collective-permute-done.5
  27.7 3.8 %collective-permute-done.4 = bf16[5,1,8,256]{3,2,0,1:T(8,128)(2,1)S(1)} collective-permute-done((bf16[5,1,8,256]{3,2,0,1:T(8,128)(2,1)S(1)}, bf16[5,1,8,256]{3,2,0,1:T(8,128)(2,1)S(1)}, u32[]{:S(2)}, u32[]{:S(2)}) %collective-permute-start.4) | collective-permute-done | bytes 20512 | tf_op jit(solution)/shard_map/ppermute | solution.py:20
  31.6 1.0 collective-permute-start.7
  32.6 2.6 %collective-permute-start.6 = (bf16[5,3,1,256]{3,1,2,0:T(4,128)(2,1)S(1)}, bf16[5,3,1,256]{3,1,2,0:T(4,128)(2,1)S(1)}, u32[]{:S(2)}, u32[]{:S(2)}) collective-permute-start(bf16[5,3,1,256]{3,1,2,0:T(4,128)(2,1)S(1)} %copy.388), channel_id=1, source_target_pairs={{0,1},{1,2},{2,3},{3,4},{4,5},{5,6},{6,7},{7,0},{8,9},{9,10},{10,1... | collective-permute-start | bytes 23048 | tf_op jit(solution)/shard_map/ppermute | solution.py:20
  35.3 1.6 %collective-permute-done.7 = bf16[5,3,1,256]{3,1,2,0:T(4,128)(2,1)S(1)} collective-permute-done((bf16[5,3,1,256]{3,1,2,0:T(4,128)(2,1)S(1)}, bf16[5,3,1,256]{3,1,2,0:T(4,128)(2,1)S(1)}, u32[]{:S(2)}, u32[]{:S(2)}) %collective-permute-start.7) | collective-permute-done | bytes 7712 | tf_op jit(solution)/shard_map/ppermute | solution.py:23
  36.9 3.0 %collective-permute-done.6 = bf16[5,3,1,256]{3,1,2,0:T(4,128)(2,1)S(1)} collective-permute-done((bf16[5,3,1,256]{3,1,2,0:T(4,128)(2,1)S(1)}, bf16[5,3,1,256]{3,1,2,0:T(4,128)(2,1)S(1)}, u32[]{:S(2)}, u32[]{:S(2)}) %collective-permute-start.6) | collective-permute-done | bytes 7712 | tf_op jit(solution)/shard_map/ppermute | solution.py:20
  42.0 3.9 %collective-permute-done.8 = bf16[5,1,8,256]{3,2,0,1:T(8,128)(2,1)S(1)} collective-permute-done((bf16[5,1,8,256]{3,2,0,1:T(8,128)(2,1)S(1)}, bf16[5,1,8,256]{3,2,0,1:T(8,128)(2,1)S(1)}, u32[]{:S(2)}, u32[]{:S(2)}) %collective-permute-start.8) | collective-permute-done | bytes 20512 | tf_op jit(solution)/shard_map/ppermute | solution.py:20
  46.1 3.5 %collective-permute-start.10 = (bf16[5,3,1,256]{3,1,2,0:T(4,128)(2,1)S(1)}, bf16[5,3,1,256]{3,1,2,0:T(4,128)(2,1)S(1)}, u32[]{:S(2)}, u32[]{:S(2)}) collective-permute-start(bf16[5,3,1,256]{3,1,2,0:T(4,128)(2,1)S(1)} %copy.400), channel_id=1, source_target_pairs={{0,1},{1,2},{2,3},{3,4},{4,5},{5,6},{6,7},{7,0},{8,9},{9,10},{10,1... | collective-permute-start | bytes 23048 | tf_op jit(solution)/shard_map/ppermute | solution.py:20
  49.6 1.6 %collective-permute-done.11 = bf16[5,3,1,256]{3,1,2,0:T(4,128)(2,1)S(1)} collective-permute-done((bf16[5,3,1,256]{3,1,2,0:T(4,128)(2,1)S(1)}, bf16[5,3,1,256]{3,1,2,0:T(4,128)(2,1)S(1)}, u32[]{:S(2)}, u32[]{:S(2)}) %collective-permute-start.11) | collective-permute-done | bytes 7712 | tf_op jit(solution)/shard_map/ppermute | solution.py:23
  51.3 2.2 %collective-permute-done.10 = bf16[5,3,1,256]{3,1,2,0:T(4,128)(2,1)S(1)} collective-permute-done((bf16[5,3,1,256]{3,1,2,0:T(4,128)(2,1)S(1)}, bf16[5,3,1,256]{3,1,2,0:T(4,128)(2,1)S(1)}, u32[]{:S(2)}, u32[]{:S(2)}) %collective-permute-start.10) | collective-permute-done | bytes 7712 | tf_op jit(solution)/shard_map/ppermute | solution.py:20
  55.4 4.0 %collective-permute-done.12 = bf16[5,1,8,256]{3,2,0,1:T(8,128)(2,1)S(1)} collective-permute-done((bf16[5,1,8,256]{3,2,0,1:T(8,128)(2,1)S(1)}, bf16[5,1,8,256]{3,2,0,1:T(8,128)(2,1)S(1)}, u32[]{:S(2)}, u32[]{:S(2)}) %collective-permute-start.12) | collective-permute-done | bytes 20512 | tf_op jit(solution)/shard_map/ppermute | solution.py:20
  59.6 3.5 %collective-permute-start.14 = (bf16[5,3,1,256]{3,1,2,0:T(4,128)(2,1)S(1)}, bf16[5,3,1,256]{3,1,2,0:T(4,128)(2,1)S(1)}, u32[]{:S(2)}, u32[]{:S(2)}) collective-permute-start(bf16[5,3,1,256]{3,1,2,0:T(4,128)(2,1)S(1)} %copy.411), channel_id=1, source_target_pairs={{0,1},{1,2},{2,3},{3,4},{4,5},{5,6},{6,7},{7,0},{8,9},{9,10},{10,1... | collective-permute-start | bytes 23048 | tf_op jit(solution)/shard_map/ppermute | solution.py:20
  63.2 1.6 %collective-permute-done.15 = bf16[5,3,1,256]{3,1,2,0:T(4,128)(2,1)S(1)} collective-permute-done((bf16[5,3,1,256]{3,1,2,0:T(4,128)(2,1)S(1)}, bf16[5,3,1,256]{3,1,2,0:T(4,128)(2,1)S(1)}, u32[]{:S(2)}, u32[]{:S(2)}) %collective-permute-start.15) | collective-permute-done | bytes 7712 | tf_op jit(solution)/shard_map/ppermute | solution.py:23
  64.8 2.2 %collective-permute-done.14 = bf16[5,3,1,256]{3,1,2,0:T(4,128)(2,1)S(1)} collective-permute-done((bf16[5,3,1,256]{3,1,2,0:T(4,128)(2,1)S(1)}, bf16[5,3,1,256]{3,1,2,0:T(4,128)(2,1)S(1)}, u32[]{:S(2)}, u32[]{:S(2)}) %collective-permute-start.14) | collective-permute-done | bytes 7712 | tf_op jit(solution)/shard_map/ppermute | solution.py:20
  68.7 2.0 %reshape.669 = bf16[8,2,2560]{2,1,0:T(2,128)(2,1)} reshape(bf16[256,5,1,4,8]{4,3,2,1,0:T(4,128)(2,1)S(1)} %bitcast.162) | data formatting | bytes 163840
  70.8 3.5 %all-to-all-start = ((bf16[8,2,2560]{2,1,0:T(2,128)(2,1)}), bf16[8,2,2560]{2,1,0:T(2,128)(2,1)S(1)}, u32[]{:S(2)}, u32[]{:S(2)}) async-start(bf16[8,2,2560]{2,1,0:T(2,128)(2,1)} %reshape.669), calls=%async_computation | async-start | bytes 163840 | tf_op jit(solution)/shard_map/all_to_all | solution.py:92
  74.3 3.4 %fusion.2 = f32[124,124]{0,1:T(8,128)S(1)} fusion(bf16[124,5,1,2048]{3,0,2,1:T(8,128)(2,1)} %param.3), kind=kOutput, calls=%fused_computation.2 | convolution fusion | flops 314900480 | bytes 2601024 | tf_op jit(solution)/shard_map/dot_general | solution.py:82
  77.7 3.3 %copy.426 = bf16[124,5,1,2048]{0,3,1,2:T(8,128)(2,1)S(1)} copy(bf16[124,5,1,2048]{3,0,2,1:T(8,128)(2,1)} %param.3) | data formatting | bytes 5079040 | tf_op args[1]
  81.0 0.8 all-to-all-done
  81.8 2.6 %reshape.670 = bf16[256,5,1,4,8]{4,3,2,1,0:T(4,128)(2,1)} reshape(bf16[8,2,2560]{2,1,0:T(2,128)(2,1)S(1)} %all-to-all-done) | data formatting | bytes 163840
  84.5 1.8 %copy.423 = bf16[4,5,1,8,8,32]{5,3,4,1,0,2:T(8,128)(2,1)S(1)} copy(bf16[4,5,1,8,8,32]{3,0,1,5,4,2:T(4,128)(2,1)} %bitcast.163) | data formatting | bytes 163840 | tf_op jit(solution)/shard_map/all_to_all | solution.py:92
  87.8 16.0 %all_to_all.28 = f32[128,1,128]{2,1,0:T(1,128)S(1)} all-to-all(f32[128,1,128]{2,1,0:T(1,128)S(1)} %copy.428), channel_id=1, replica_groups=mesh['wide'=16,'narrow'=8] {'wide','narrow'}, dimensions={0} | all-to-all | bytes 131072 | tf_op jit(solution)/shard_map/all_to_all | solution.py:111
  104.0 13.8 %all_to_all.29 = f32[128,1,128]{2,1,0:T(1,128)S(1)} all-to-all(f32[128,1,128]{2,1,0:T(1,128)S(1)} %broadcast_in_dim.3), channel_id=1, replica_groups=mesh['wide'=16,'narrow'=8] {'wide','narrow'}, dimensions={0} | all-to-all | bytes 131072 | tf_op jit(solution)/shard_map/all_to_all | solution.py:114
  117.9 11.7 %cholesky.18 = f32[128,128]{1,0:T(8,128)S(1)} custom-call(f32[128,128]{1,0:T(8,128)S(1)} %fusion.6), custom_call_target="Cholesky" | custom-call | tf_op jit(solution)/shard_map/jit(cholesky)/cholesky | solution.py:116
  (138 shorter events, 15.4 us)
Async XLA Ops:
  1.4 9.2 %collective-permute-start.1 = (bf16[5,1,8,256]{3,2,1,0:T(8,128)(2,1)S(1)}, bf16[5,1,8,256]{3,2,1,0:T(8,128)(2,1)S(1)}, u32[]{:S(2)}, u32[]{:S(2)}) collective-permute-start(bf16[5,1,8,256]{3,2,1,0:T(8,128)(2,1)S(1)} %convert_element_type.30), channel_id=1, source_target_pairs={{8,0},{16,8},{24,16},{32,24},{40,32},{48,40},{56,48},{64,56},{72,6... | collective-permute-start | bytes 61448 | tf_op jit(solution)/shard_map/ppermute | solution.py:23
  6.0 5.3 %collective-permute-start = (bf16[5,1,8,256]{3,2,1,0:T(8,128)(2,1)S(1)}, bf16[5,1,8,256]{3,2,1,0:T(8,128)(2,1)S(1)}, u32[]{:S(2)}, u32[]{:S(2)}) collective-permute-start(bf16[5,1,8,256]{3,2,1,0:T(8,128)(2,1)S(1)} %convert_element_type.30), channel_id=1, source_target_pairs={{0,8},{8,16},{16,24},{24,32},{32,40},{40,48},{48,56},{56,64},{64,7... | collective-permute-start | bytes 61448 | tf_op jit(solution)/shard_map/ppermute | solution.py:20
  6.7 33.5 %copy-start = (f32[5,1,8,256]{3,2,1,0:T(8,128)S(1)}, f32[5,1,8,256]{3,2,1,0:T(8,128)}, u32[]{:S(2)}) copy-start(f32[5,1,8,256]{3,2,1,0:T(8,128)} %param.2) | copy-start | bytes 122884
  11.4 6.5 %collective-permute-start.3 = (bf16[5,3,1,256]{3,1,2,0:T(4,128)(2,1)S(1)}, bf16[5,3,1,256]{3,1,2,0:T(4,128)(2,1)S(1)}, u32[]{:S(2)}, u32[]{:S(2)}) collective-permute-start(bf16[5,3,1,256]{3,1,2,0:T(4,128)(2,1)S(1)} %copy.436), channel_id=1, source_target_pairs={{1,0},{2,1},{3,2},{4,3},{5,4},{6,5},{7,6},{0,7},{9,8},{10,9},{11,1... | collective-permute-start | bytes 23048 | tf_op jit(solution)/shard_map/ppermute | solution.py:23
  16.6 7.3 %collective-permute-start.2 = (bf16[5,3,1,256]{3,1,2,0:T(4,128)(2,1)S(1)}, bf16[5,3,1,256]{3,1,2,0:T(4,128)(2,1)S(1)}, u32[]{:S(2)}, u32[]{:S(2)}) collective-permute-start(bf16[5,3,1,256]{3,1,2,0:T(4,128)(2,1)S(1)} %copy.435), channel_id=1, source_target_pairs={{0,1},{1,2},{2,3},{3,4},{4,5},{5,6},{6,7},{7,0},{8,9},{9,10},{10,1... | collective-permute-start | bytes 23048 | tf_op jit(solution)/shard_map/ppermute | solution.py:20
  25.1 2.7 %collective-permute-start.5 = (bf16[5,1,8,256]{3,2,0,1:T(8,128)(2,1)S(1)}, bf16[5,1,8,256]{3,2,0,1:T(8,128)(2,1)S(1)}, u32[]{:S(2)}, u32[]{:S(2)}) collective-permute-start(bf16[5,1,8,256]{3,2,0,1:T(8,128)(2,1)S(1)} %get-tuple-element.65), channel_id=1, source_target_pairs={{8,0},{16,8},{24,16},{32,24},{40,32},{48,40},{56,48},{64,56},{72,6... | collective-permute-start | bytes 61448 | tf_op jit(solution)/shard_map/ppermute | solution.py:23
  26.3 5.3 %collective-permute-start.4 = (bf16[5,1,8,256]{3,2,0,1:T(8,128)(2,1)S(1)}, bf16[5,1,8,256]{3,2,0,1:T(8,128)(2,1)S(1)}, u32[]{:S(2)}, u32[]{:S(2)}) collective-permute-start(bf16[5,1,8,256]{3,2,0,1:T(8,128)(2,1)S(1)} %get-tuple-element.65), channel_id=1, source_target_pairs={{0,8},{8,16},{16,24},{24,32},{32,40},{40,48},{48,56},{56,64},{64,7... | collective-permute-start | bytes 61448 | tf_op jit(solution)/shard_map/ppermute | solution.py:20
  31.6 5.2 %collective-permute-start.7 = (bf16[5,3,1,256]{3,1,2,0:T(4,128)(2,1)S(1)}, bf16[5,3,1,256]{3,1,2,0:T(4,128)(2,1)S(1)}, u32[]{:S(2)}, u32[]{:S(2)}) collective-permute-start(bf16[5,3,1,256]{3,1,2,0:T(4,128)(2,1)S(1)} %copy.389), channel_id=1, source_target_pairs={{1,0},{2,1},{3,2},{4,3},{5,4},{6,5},{7,6},{0,7},{9,8},{10,9},{11,1... | collective-permute-start | bytes 23048 | tf_op jit(solution)/shard_map/ppermute | solution.py:23
  32.6 7.3 %collective-permute-start.6 = (bf16[5,3,1,256]{3,1,2,0:T(4,128)(2,1)S(1)}, bf16[5,3,1,256]{3,1,2,0:T(4,128)(2,1)S(1)}, u32[]{:S(2)}, u32[]{:S(2)}) collective-permute-start(bf16[5,3,1,256]{3,1,2,0:T(4,128)(2,1)S(1)} %copy.388), channel_id=1, source_target_pairs={{0,1},{1,2},{2,3},{3,4},{4,5},{5,6},{6,7},{7,0},{8,9},{9,10},{10,1... | collective-permute-start | bytes 23048 | tf_op jit(solution)/shard_map/ppermute | solution.py:20
  40.5 1.5 %collective-permute-start.9 = (bf16[5,1,8,256]{3,2,0,1:T(8,128)(2,1)S(1)}, bf16[5,1,8,256]{3,2,0,1:T(8,128)(2,1)S(1)}, u32[]{:S(2)}, u32[]{:S(2)}) collective-permute-start(bf16[5,1,8,256]{3,2,0,1:T(8,128)(2,1)S(1)} %fusion.78), channel_id=1, source_target_pairs={{8,0},{16,8},{24,16},{32,24},{40,32},{48,40},{56,48},{64,56},{72,6... | collective-permute-start | bytes 61448 | tf_op jit(solution)/shard_map/ppermute | solution.py:23
  40.6 5.4 %collective-permute-start.8 = (bf16[5,1,8,256]{3,2,0,1:T(8,128)(2,1)S(1)}, bf16[5,1,8,256]{3,2,0,1:T(8,128)(2,1)S(1)}, u32[]{:S(2)}, u32[]{:S(2)}) collective-permute-start(bf16[5,1,8,256]{3,2,0,1:T(8,128)(2,1)S(1)} %fusion.78), channel_id=1, source_target_pairs={{0,8},{8,16},{16,24},{24,32},{32,40},{40,48},{48,56},{56,64},{64,7... | collective-permute-start | bytes 61448 | tf_op jit(solution)/shard_map/ppermute | solution.py:20
  46.0 5.2 %collective-permute-start.11 = (bf16[5,3,1,256]{3,1,2,0:T(4,128)(2,1)S(1)}, bf16[5,3,1,256]{3,1,2,0:T(4,128)(2,1)S(1)}, u32[]{:S(2)}, u32[]{:S(2)}) collective-permute-start(bf16[5,3,1,256]{3,1,2,0:T(4,128)(2,1)S(1)} %copy.401), channel_id=1, source_target_pairs={{1,0},{2,1},{3,2},{4,3},{5,4},{6,5},{7,6},{0,7},{9,8},{10,9},{11,1... | collective-permute-start | bytes 23048 | tf_op jit(solution)/shard_map/ppermute | solution.py:23
  46.1 7.4 %collective-permute-start.10 = (bf16[5,3,1,256]{3,1,2,0:T(4,128)(2,1)S(1)}, bf16[5,3,1,256]{3,1,2,0:T(4,128)(2,1)S(1)}, u32[]{:S(2)}, u32[]{:S(2)}) collective-permute-start(bf16[5,3,1,256]{3,1,2,0:T(4,128)(2,1)S(1)} %copy.400), channel_id=1, source_target_pairs={{0,1},{1,2},{2,3},{3,4},{4,5},{5,6},{6,7},{7,0},{8,9},{9,10},{10,1... | collective-permute-start | bytes 23048 | tf_op jit(solution)/shard_map/ppermute | solution.py:20
  53.9 1.6 %collective-permute-start.13 = (bf16[5,1,8,256]{3,2,0,1:T(8,128)(2,1)S(1)}, bf16[5,1,8,256]{3,2,0,1:T(8,128)(2,1)S(1)}, u32[]{:S(2)}, u32[]{:S(2)}) collective-permute-start(bf16[5,1,8,256]{3,2,0,1:T(8,128)(2,1)S(1)} %get-tuple-element.31), channel_id=1, source_target_pairs={{8,0},{16,8},{24,16},{32,24},{40,32},{48,40},{56,48},{64,56},{72,6... | collective-permute-start | bytes 61448 | tf_op jit(solution)/shard_map/ppermute | solution.py:23
  54.0 5.5 %collective-permute-start.12 = (bf16[5,1,8,256]{3,2,0,1:T(8,128)(2,1)S(1)}, bf16[5,1,8,256]{3,2,0,1:T(8,128)(2,1)S(1)}, u32[]{:S(2)}, u32[]{:S(2)}) collective-permute-start(bf16[5,1,8,256]{3,2,0,1:T(8,128)(2,1)S(1)} %get-tuple-element.31), channel_id=1, source_target_pairs={{0,8},{8,16},{16,24},{24,32},{32,40},{40,48},{48,56},{56,64},{64,7... | collective-permute-start | bytes 61448 | tf_op jit(solution)/shard_map/ppermute | solution.py:20
  59.5 5.2 %collective-permute-start.15 = (bf16[5,3,1,256]{3,1,2,0:T(4,128)(2,1)S(1)}, bf16[5,3,1,256]{3,1,2,0:T(4,128)(2,1)S(1)}, u32[]{:S(2)}, u32[]{:S(2)}) collective-permute-start(bf16[5,3,1,256]{3,1,2,0:T(4,128)(2,1)S(1)} %copy.412), channel_id=1, source_target_pairs={{1,0},{2,1},{3,2},{4,3},{5,4},{6,5},{7,6},{0,7},{9,8},{10,9},{11,1... | collective-permute-start | bytes 23048 | tf_op jit(solution)/shard_map/ppermute | solution.py:23
  59.6 7.4 %collective-permute-start.14 = (bf16[5,3,1,256]{3,1,2,0:T(4,128)(2,1)S(1)}, bf16[5,3,1,256]{3,1,2,0:T(4,128)(2,1)S(1)}, u32[]{:S(2)}, u32[]{:S(2)}) collective-permute-start(bf16[5,3,1,256]{3,1,2,0:T(4,128)(2,1)S(1)} %copy.411), channel_id=1, source_target_pairs={{0,1},{1,2},{2,3},{3,4},{4,5},{5,6},{6,7},{7,0},{8,9},{9,10},{10,1... | collective-permute-start | bytes 23048 | tf_op jit(solution)/shard_map/ppermute | solution.py:20
  70.8 11.1 %all-to-all-start = ((bf16[8,2,2560]{2,1,0:T(2,128)(2,1)}), bf16[8,2,2560]{2,1,0:T(2,128)(2,1)S(1)}, u32[]{:S(2)}, u32[]{:S(2)}) async-start(bf16[8,2,2560]{2,1,0:T(2,128)(2,1)} %reshape.669), calls=%async_computation | async-start | bytes 163840 | tf_op jit(solution)/shard_map/all_to_all | solution.py:92

commit v2 on v0

v2 whole, which is shorter than its diff:
```python
import functools

import jax
import jax.numpy as jnp
from jax import lax
from jax.experimental import pallas as pl
from jax.experimental.pallas import tpu as pltpu
from jax.sharding import PartitionSpec as P

GAMMA = 1.4
TIME_STEP = 0.25
VISCOSITY = 0.15
MEANS = (1.0, 0.0, 0.0, 0.0, 2.5)
HALO = 4
WIDE = 16
NARROW = 8
DEVICES = WIDE * NARROW
MODES = 124
COLS = 128
ZPART = 32
WINDOW = ZPART + 2 * HALO
YPART = 8
NY = 64
INVERSE_CELLS = 1.0 / 262144.0
EVERYWHERE = ("wide", "narrow")
F32 = jnp.float32
BF16 = jnp.bfloat16


def lanes(shape):
    return lax.broadcasted_iota(jnp.int32, shape, len(shape) - 1)


def pack_kernel(fields_ref, modes_ref, out_ref, gram_ref):
    comp = pl.program_id(0)
    block = modes_ref[0]
    product = lax.dot_general(
        block, block, (((1,), (1,)), ((), ())), preferred_element_type=F32
    )

    @pl.when(comp == 0)
    def _():
        gram_ref[...] = jnp.zeros_like(gram_ref)

    gram_ref[0:MODES, 0:MODES] += product

    @pl.when(comp == pl.num_programs(0) - 1)
    def _():
        gram = gram_ref[...]
        high = gram.astype(BF16).astype(F32)
        rest = gram - high
        middle = rest.astype(BF16).astype(F32)
        low = rest - middle
        lane = lanes((YPART, 128))
        lane_full = lanes((COLS, 128))
        shifted = [fields_ref[c] - MEANS[c] for c in range(5)]
        for n in range(NARROW):
            def window(c, place):
                amount = (place * WINDOW + HALO - ZPART * n) % 256
                moved = pltpu.roll(shifted[c], amount, 1) if amount else shifted[c]
                return moved[:, 0:128]

            first = jnp.where(
                lane < WINDOW,
                window(0, 0),
                jnp.where(lane < 2 * WINDOW, window(1, 1), window(2, 2)),
            )
            first = jnp.where(lane < 3 * WINDOW, first, 0.0)
            second = jnp.where(lane < WINDOW, window(3, 0), window(4, 1))

            def turned(x, place):
                amount = (place - 16 * n) % 128
                return pltpu.roll(x, amount, 1) if amount else x

            parts = jnp.where(
                lane_full < 96,
                turned(high, 80),
                jnp.where(lane_full < 112, turned(middle, 96), turned(low, 112)),
            ).reshape(WIDE, YPART, 128)
            lower = jnp.broadcast_to(first[None], (WIDE, YPART, 128))
            upper = jnp.where(lane[None] < 2 * WINDOW, second[None], parts)
            piece = jnp.concatenate([lower, upper], axis=1).astype(BF16)
            out_ref[:, n] = piece


def pack(fields, modes):
    return pl.pallas_call(
        pack_kernel,
        grid=(5,),
        in_specs=[
            pl.BlockSpec((5, YPART, 256), lambda c: (0, 0, 0)),
            pl.BlockSpec((1, MODES, 2048), lambda c: (c, 0, 0)),
        ],
        out_specs=pl.BlockSpec((WIDE, NARROW, 16, 128), lambda c: (0, 0, 0, 0)),
        out_shape=jax.ShapeDtypeStruct((WIDE, NARROW, 16, 128), BF16),
        scratch_shapes=[pltpu.VMEM((COLS, 128), F32)],
        name="pack",
    )(fields, modes)


def up(x, axis):
    return pltpu.roll(x, x.shape[axis] - 1, axis)


def down(x, axis):
    return pltpu.roll(x, 1, axis)


def fluxes(u, directions):
    density, m1, m2, m3, energy = u
    inverse = 1.0 / density
    v = (m1 * inverse, m2 * inverse, m3 * inverse)
    products = {}
    momenta = (m1, m2, m3)
    for i in range(3):
        products[(i, i)] = momenta[i] * v[i]
    pressure = (GAMMA - 1.0) * (
        energy - 0.5 * (products[(0, 0)] + products[(1, 1)] + products[(2, 2)])
    )
    total = energy + pressure
    out = []
    for d in directions:
        row = [momenta[d]]
        for i in range(3):
            if i == d:
                row.append(products[(d, d)] + pressure)
            else:
                key = (min(i, d), max(i, d))
                if key not in products:
                    products[key] = momenta[key[0]] * v[key[1]]
                row.append(products[key])
        row.append(total * v[d])
        out.append(row)
    return out


def section(load, planes):
    ahead, behind, partial = {}, {}, {}
    centre = 1.0 - 6.0 * VISCOSITY * TIME_STEP
    soft = VISCOSITY * TIME_STEP
    half = 0.5 * TIME_STEP
    wanted = set(planes)
    everything = sorted({p + s for p in planes for s in (-1, 0, 1)})
    result = {}
    for p in everything:
        u = load(p)
        inner = p in wanted
        rows = fluxes(u, (0, 1, 2) if inner else (0,))
        smooth = [soft * x for x in u]
        ahead[p] = [smooth[c] - half * rows[0][c] for c in range(5)]
        behind[p] = [smooth[c] + half * rows[0][c] for c in range(5)]
        if inner:
            total = []
            for c in range(5):
                y, z = half * rows[1][c], half * rows[2][c]
                total.append(
                    centre * u[c]
                    + (up(smooth[c] - y, 0) + down(smooth[c] + y, 0))
                    + (up(smooth[c] - z, 1) + down(smooth[c] + z, 1))
                )
            partial[p] = total
        q = p - 1
        if q in wanted:
            result[q] = [partial[q][c] + (ahead[q + 1][c] + behind[q - 1][c]) for c in range(5)]
            yield q, result[q]


def step_kernel(w_ref, recv_ref, modes_hbm, whole_ref, back_ref, one, two, modes_ref, turn_ref, sem):
    copies = [
        pltpu.make_async_copy(modes_hbm.at[c], modes_ref.at[c], sem.at[c]) for c in range(5)
    ]
    for copy in copies:
        copy.start()
    w = w_ref[0]
    lane = lanes((NY, 128))

    def load(p):
        start = lax.rem(w + (p + WIDE), WIDE) * NARROW
        block = recv_ref[pl.ds(start, NARROW)].astype(F32)
        lower = block[:, 0:8].reshape(NY, 128)
        upper = block[:, 8:16].reshape(NY, 128)
        return [
            lower + MEANS[0],
            pltpu.roll(lower, 128 - WINDOW, 1),
            pltpu.roll(lower, 128 - 2 * WINDOW, 1),
            upper,
            pltpu.roll(upper, 128 - WINDOW, 1) + MEANS[4],
        ]

    terms = recv_ref[:, 8:16, :].astype(F32)
    summed = jnp.sum(terms, axis=0)
    block = (pltpu.roll(summed, 16, 1) + pltpu.roll(summed, 32, 1)) + pltpu.roll(summed, 48, 1)

    packed = [jnp.zeros((NY, 128), F32) for _ in range(5)]
    valid = lane < ZPART

    def keep(index, u):
        for c in range(5):
            value = pltpu.roll(u[c], 128 - HALO, 1) if index == 0 else pltpu.roll(
                u[c], ZPART * index - HALO, 1
            )
            inside = (lane >= ZPART * index) & (lane < ZPART * (index + 1))
            packed[c] = jnp.where(inside, value, packed[c])

    def stored(ref, offset):
        return lambda p: [ref[p + offset, c] for c in range(5)]

    for q, v in section(load, range(-3, 4)):
        for c in range(5):
            one[q + 3, c] = v[c]
        if q == 0:
            keep(0, v)
    for q, v in section(stored(one, 3), range(-2, 3)):
        u = load(q)
        new = [0.5 * (u[c] + v[c]) for c in range(5)]
        for c in range(5):
            two[q + 2, c] = new[c]
        if q == 0:
            keep(1, new)
    for q, v in section(stored(two, 2), range(-1, 2)):
        for c in range(5):
            one[q + 1, c] = v[c]
        if q == 0:
            keep(2, v)
    for q, v in section(stored(one, 1), range(0, 1)):
        new = [0.5 * (two[2, c] + v[c]) for c in range(5)]
        keep(3, new)
        back = [None] * 5
        spread = jnp.zeros((NY, 128), F32)
        for c in range(4):
            value = pltpu.roll(new[c], 128 - HALO, 1) if c == 0 else pltpu.roll(
                new[c], ZPART * c - HALO, 1
            )
            inside = (lane >= ZPART * c) & (lane < ZPART * (c + 1))
            spread = jnp.where(inside, value, spread)
        last = jnp.where(valid, pltpu.roll(new[4], 128 - HALO, 1), 0.0)
        back_ref[:, 0:8, :] = spread.reshape(NARROW, YPART, 128)
        back_ref[:, 8:16, :] = last.reshape(NARROW, YPART, 128)

    cross = jnp.zeros((4, MODES), F32)
    square = jnp.zeros((4, 4), F32)
    contract = (((1,), (1,)), ((), ()))
    for c in range(5):
        rounded = packed[c].astype(BF16).astype(F32)
        pair = jnp.concatenate([rounded, pltpu.roll(rounded, 127, 1)], axis=0)
        turn_ref[c] = pair.T
    for c in range(5):
        chunks = [turn_ref[c, pl.ds(2 * k, 4, stride=ZPART), :] for k in range(16)]
        rows = jnp.concatenate(chunks, axis=1).astype(BF16)
        copies[c].wait()
        cross += lax.dot_general(rows, modes_ref[c], contract, preferred_element_type=F32)
        square += lax.dot_general(rows, rows, contract, preferred_element_type=F32)
    top = jnp.concatenate([cross, square], axis=1)
    lane8 = lanes((4, 128))
    bottom = jnp.where(lane8 < 16, block[0:4], pltpu.roll(block, 16, 1)[4:8])
    bottom = jnp.where(lane8 < 32, bottom, 0.0)
    piece = jnp.concatenate([top, bottom], axis=0) * INVERSE_CELLS
    whole_ref[...] = jnp.broadcast_to(piece[None], whole_ref.shape)


def steps(w, recv, modes):
    return pl.pallas_call(
        step_kernel,
        in_specs=[
            pl.BlockSpec(memory_space=pltpu.SMEM),
            pl.BlockSpec(memory_space=pltpu.VMEM),
            pl.BlockSpec(memory_space=pl.ANY),
        ],
        out_specs=[
            pl.BlockSpec(memory_space=pltpu.VMEM),
            pl.BlockSpec(memory_space=pltpu.VMEM),
        ],
        out_shape=[
            jax.ShapeDtypeStruct((DEVICES, 8, 128), F32),
            jax.ShapeDtypeStruct((NARROW, 16, 128), F32),
        ],
        scratch_shapes=[
            pltpu.VMEM((7, 5, NY, 128), F32),
            pltpu.VMEM((5, 5, NY, 128), F32),
            pltpu.VMEM((5, MODES, 2048), BF16),
            pltpu.VMEM((5, 128, 128), F32),
            pltpu.SemaphoreType.DMA((5,)),
        ],
        name="steps",
    )(w, recv, modes)


def gram_kernel(whole_ref, gram_ref):
    cross = jnp.sum(whole_ref[:, 0:4, :], axis=0)
    lane = lanes((4, 128))
    for a in range(16):
        low = jnp.zeros((4, 128), F32)
        high = jnp.zeros((4, 128), F32)
        for b in range(8):
            part = whole_ref[8 * a + b, 4:8, :]
            inside = (lane >= 16 * b) & (lane < 16 * (b + 1))
            first = pltpu.roll(part, 16 * b, 1) if b else part
            second = pltpu.roll(part, (16 * b - 16) % 128, 1) if b != 1 else part
            low = jnp.where(inside, first, low)
            high = jnp.where(inside, second, high)
        if a == 15:
            high = cross
        gram_ref[8 * a : 8 * a + 8, :] = jnp.concatenate([low, high], axis=0)


def gather_gram(whole):
    return pl.pallas_call(
        gram_kernel,
        out_shape=jax.ShapeDtypeStruct((COLS, 128), F32),
        name="gram",
    )(whole)


def owner_kernel(back_ref, out_ref):
    lane = lanes((YPART, 256))
    for c in range(5):
        total = jnp.zeros((YPART, 256), F32)
        place = ZPART * (c % 4)
        row = 8 * (c // 4)
        for n in range(NARROW):
            part = back_ref[n, row : row + 8, :]
            part = jnp.concatenate([part, part], axis=1)
            amount = (ZPART * n - place) % 256
            part = pltpu.roll(part, amount, 1) if amount else part
            inside = (lane >= ZPART * n) & (lane < ZPART * (n + 1))
            total = jnp.where(inside, part, total)
        out_ref[c] = total


def owner(back):
    return pl.pallas_call(
        owner_kernel,
        out_shape=jax.ShapeDtypeStruct((5, YPART, 256), F32),
        name="owner",
    )(back)


def local(fields, prior_modes):
    modes = jnp.transpose(prior_modes[:, :, 0, :], (1, 0, 2))
    w = lax.axis_index("wide").astype(jnp.int32).reshape(1)
    sent = pack(fields[:, 0], modes).reshape(DEVICES, 16, 128)
    recv = lax.all_to_all(sent, EVERYWHERE, split_axis=0, concat_axis=0, tiled=True)
    whole, back = steps(w, recv, modes)
    whole = lax.all_to_all(whole, EVERYWHERE, split_axis=0, concat_axis=0, tiled=True)
    back = lax.all_to_all(back, "narrow", split_axis=0, concat_axis=0, tiled=True)
    state = owner(back)[:, None]
    gram = gather_gram(whole)
    factor = jnp.linalg.cholesky(gram, symmetrize_input=False).T
    return (state, factor)


def solution(mesh):
    placed = (P(None, "wide", "narrow", None), P(None, None, "wide", "narrow"))
    return jax.shard_map(
        local,
        mesh=mesh,
        in_specs=placed,
        out_specs=(P(None, "wide", "narrow", None), P()),
        check_vma=False,
    )
```

time: 257 us -> 87.1 us (0.34); the launches traced: 253 us -> 86.5 us
  waiting for transfers between devices: 170 us -> 25.2 us
  Pallas kernels: 0 us -> 17 us
  local copies, waits for them, and re-layouts: 16.3 us -> 2.3 us
  between operations: 14.6 us -> 0.68 us
  blocking collectives: 0 us -> 11.7 us
  starting transfers between devices: 26.5 us -> 15.8 us
  other arithmetic: 21.4 us -> 13.9 us
  matrix products: 4.11 us -> 0 us
    psum x1 -> x0, waiting for transfers between devices: 135 us -> none  [local(): gram_whole = lax.psum(gram_local, ('wide', 'narrow'))]
    ppermute x16 -> x0, waiting for transfers between devices: 33.7 us -> none  [the longest x8 25.7 us: extended(): lax.ppermute(lax.slice_in_dim(block, block.shape[dim] - width, None, axis...]
    all_to_all x1 -> x2, waiting for transfers between devices: 0.79 us -> 25.2 us  [the longest x1 13.4 us: local(): lax.all_to_all(sent, EVERYWHERE, split_axis=0, concat_axis=0, tiled=True)]
    ppermute x16 -> x0, starting transfers between devices: 22.9 us -> none  [the longest x8 12.2 us: extended(): lax.ppermute(lax.slice_in_dim(block, 0, width, axis=dim), axis, backward)]
    pallas_call x0 -> x4, Pallas kernels: none -> 17 us  [the longest x1 8.3 us: steps(): pl.pallas_call(step_kernel, in_specs=[pl.BlockSpec(memory_space=pltpu.SME...]
    all_to_all x1 -> x2, starting transfers between devices: 3.36 us -> 15.8 us  [the longest x1 11.2 us: local(): lax.all_to_all(sent, EVERYWHERE, split_axis=0, concat_axis=0, tiled=True)]
    all_to_all x0 -> x1, blocking collectives: none -> 11.7 us  [local(): lax.all_to_all(back, 'narrow', split_axis=0, concat_axis=0, tiled=True)]
    unnamed x16 -> x5, local copies, waits for them, and re-layouts: 9.47 us -> 2.3 us
  transfers between devices with their start and end apart: 18 -> 2, of which waited for: 17 -> 2; matrix products, arithmetic and copies ran while one was open for 5% -> 0% of each run, Pallas kernels for 0% -> 2%
where the time goes in v2:
time: 87.1 us; the launch traced here: 86.5 us
  waiting for transfers between devices  25.2 us (29%)
  Pallas kernels  17 us (20%)
  starting transfers between devices  15.8 us (18%)
  other arithmetic  13.9 us (16%)
  blocking collectives  11.7 us (13%)
  local copies, waits for them, and re-layouts  2.3 us (3%)
    all_to_all x1, waiting for transfers between devices, local(): lax.all_to_all(sent, EVERYWHERE, split_axis=0, concat_axis=0, tiled=True)  13.4 us
    another operation x3, other arithmetic, local(): factor = jnp.linalg.cholesky(gram, symmetrize_input=False).T  13.2 us
    all_to_all x1, waiting for transfers between devices, local(): lax.all_to_all(whole, EVERYWHERE, split_axis=0, concat_axis=0, tiled=True)  11.8 us
    all_to_all x1, blocking collectives, local(): lax.all_to_all(back, 'narrow', split_axis=0, concat_axis=0, tiled=True)  11.7 us
    all_to_all x1, starting transfers between devices, local(): lax.all_to_all(sent, EVERYWHERE, split_axis=0, concat_axis=0, tiled=True)  11.2 us
    pallas_call x1, Pallas kernels, steps(): pl.pallas_call(step_kernel, in_specs=[pl.BlockSpec(memory_space=pltpu.SME...  8.3 us
    pallas_call x1, Pallas kernels, pack(): pl.pallas_call(pack_kernel, grid=(5,), in_specs=[pl.BlockSpec((5, YPART,...  5.14 us
    all_to_all x1, starting transfers between devices, local(): lax.all_to_all(whole, EVERYWHERE, split_axis=0, concat_axis=0, tiled=True)  4.6 us
  transfers between devices with their start and end apart: 2, of which 2 were waited for; matrix products, arithmetic and copies ran while one was open for 0% of the time, Pallas kernels for 2%

profile of v2, /device:TPU:0, one launch (start us, length us, event | category | flops | bytes accessed | tf_op | source)
XLA Modules:
  0.0 86.5 jit_solution(5640250778267547131)
XLA Ops:
  0.6 5.1 %pack.1 = bf16[16,8,16,128]{3,2,1,0:T(8,128)(2,1)} custom-call(f32[5,8,256]{2,1,0:T(8,128)} %bitcast.15, bf16[5,124,2048]{2,1,0:T(8,128)(2,1)} %bitcast.11), custom_call_target="tpu_custom_call" | custom-call | tf_op jit(solution)/shard_map/pack/pallas_call | solution.py:87
  5.8 11.2 %all-to-all-start = ((bf16[128,16,128]{2,1,0:T(8,128)(2,1)}), bf16[128,16,128]{2,1,0:T(8,128)(2,1)S(1)}, u32[]{:S(2)}, u32[]{:S(2)}) async-start(bf16[128,16,128]{2,1,0:T(8,128)(2,1)} %bitcast.13), calls=%async_computation | async-start | bytes 1048576 | tf_op jit(solution)/shard_map/all_to_all | solution.py:342
  16.9 13.4 %all-to-all-done.recv_ref = bf16[128,16,128]{2,1,0:T(8,128)(2,1)S(1)} async-done(((bf16[128,16,128]{2,1,0:T(8,128)(2,1)}), bf16[128,16,128]{2,1,0:T(8,128)(2,1)S(1)}, u32[]{:S(2)}, u32[]{:S(2)}) %all-to-all-start) | async-done | bytes 524320 | tf_op jit(solution)/shard_map/all_to_all | solution.py:342
  30.3 0.0 copy-start.1
  30.3 0.8 copy-done.1
  31.1 8.3 %steps.1 = (f32[128,8,128]{2,1,0:T(8,128)}, f32[8,16,128]{2,1,0:T(8,128)}) custom-call(s32[1]{0:T(128)} %bitcast.w_ref, bf16[128,16,128]{2,1,0:T(8,128)(2,1)} %copy-done.1, bf16[5,124,2048]{2,1,0:T(8,128)(2,1)} %bitcast.12), custom_call_target="tpu_custom_call" | custom-call | tf_op jit(solution)/shard_map/steps/pallas_call | solution.py:262
  39.4 11.7 %all_to_all.15.back_ref = f32[8,16,128]{2,1,0:T(8,128)} all-to-all(f32[8,16,128]{2,1,0:T(8,128)} %get-tuple-element.4), channel_id=1, replica_groups=mesh['wide'=16,'narrow'=8] {'narrow'}, dimensions={0} | all-to-all | bytes 131072 | tf_op jit(solution)/shard_map/all_to_all | solution.py:345
  51.1 4.6 %all-to-all-start.2 = ((f32[128,8,128]{2,1,0:T(8,128)}), f32[128,8,128]{2,1,0:T(8,128)S(1)}, u32[]{:S(2)}, u32[]{:S(2)}) async-start(f32[128,8,128]{2,1,0:T(8,128)} %get-tuple-element.5), calls=%async_computation.2 | async-start | bytes 1048576 | tf_op jit(solution)/shard_map/all_to_all | solution.py:344
  55.7 1.6 %owner.1 = f32[5,8,256]{2,1,0:T(8,128)} custom-call(f32[8,16,128]{2,1,0:T(8,128)} %all_to_all.15.back_ref), custom_call_target="tpu_custom_call" | custom-call | tf_op jit(solution)/shard_map/owner/pallas_call | solution.py:331
  57.3 11.8 %all-to-all-done.2.whole_ref = f32[128,8,128]{2,1,0:T(8,128)S(1)} async-done(((f32[128,8,128]{2,1,0:T(8,128)}), f32[128,8,128]{2,1,0:T(8,128)S(1)}, u32[]{:S(2)}, u32[]{:S(2)}) %all-to-all-start.2) | async-done | bytes 524320 | tf_op jit(solution)/shard_map/all_to_all | solution.py:344
  69.1 0.0 copy-start
  69.1 0.8 copy-done
  69.9 2.0 %gram.1 = f32[128,128]{1,0:T(8,128)} custom-call(f32[128,8,128]{2,1,0:T(8,128)} %copy-done), custom_call_target="tpu_custom_call" | custom-call | tf_op jit(solution)/shard_map/gram/pallas_call | solution.py:307
  71.9 12.5 %cholesky.18 = f32[128,128]{1,0:T(8,128)S(1)} custom-call(f32[128,128]{1,0:T(8,128)} %gram.1), custom_call_target="Cholesky" | custom-call | tf_op jit(solution)/shard_map/jit(cholesky)/cholesky | solution.py:348
  84.4 0.6 compare_reduce_fusion
  85.1 0.7 select_bitcast_fusion
  85.7 0.7 copy.5
  (1 shorter events, 0.0 us)
Async XLA Ops:
  5.8 24.5 %all-to-all-start = ((bf16[128,16,128]{2,1,0:T(8,128)(2,1)}), bf16[128,16,128]{2,1,0:T(8,128)(2,1)S(1)}, u32[]{:S(2)}, u32[]{:S(2)}) async-start(bf16[128,16,128]{2,1,0:T(8,128)(2,1)} %bitcast.13), calls=%async_computation | async-start | bytes 1048576 | tf_op jit(solution)/shard_map/all_to_all | solution.py:342
  30.3 0.8 copy-start.1
  51.1 18.0 %all-to-all-start.2 = ((f32[128,8,128]{2,1,0:T(8,128)}), f32[128,8,128]{2,1,0:T(8,128)S(1)}, u32[]{:S(2)}, u32[]{:S(2)}) async-start(f32[128,8,128]{2,1,0:T(8,128)} %get-tuple-element.5), calls=%async_computation.2 | async-start | bytes 1048576 | tf_op jit(solution)/shard_map/all_to_all | solution.py:344
  69.1 0.8 copy-start

commit v3 on v2

--- a/solution.py
+++ b/solution.py
@@ -1,11 +1,10 @@
-import functools
-
 import jax
 import jax.numpy as jnp
 from jax import lax
 from jax.experimental import pallas as pl
 from jax.experimental.pallas import tpu as pltpu
 from jax.sharding import PartitionSpec as P
+
 
 GAMMA = 1.4
 TIME_STEP = 0.25
@@ -95,6 +94,7 @@
         out_shape=jax.ShapeDtypeStruct((WIDE, NARROW, 16, 128), BF16),
         scratch_shapes=[pltpu.VMEM((COLS, 128), F32)],
         name="pack",
+        compiler_params=pltpu.CompilerParams(vmem_limit_bytes=16 * 2**20),
     )(fields, modes)
 
 
@@ -225,7 +225,6 @@
     for q, v in section(stored(one, 1), range(0, 1)):
         new = [0.5 * (two[2, c] + v[c]) for c in range(5)]
         keep(3, new)
-        back = [None] * 5
         spread = jnp.zeros((NY, 128), F32)
         for c in range(4):
             value = pltpu.roll(new[c], 128 - HALO, 1) if c == 0 else pltpu.roll(
@@ -282,12 +281,56 @@
             pltpu.SemaphoreType.DMA((5,)),
         ],
         name="steps",
+        compiler_params=pltpu.CompilerParams(vmem_limit_bytes=24 * 2**20),
     )(w, recv, modes)
+
+
+def along_lanes(x, j):
+    return jnp.broadcast_to(x[:, j : j + 1], x.shape)
+
+
+def along_rows(x, i):
+    return jnp.broadcast_to(x[i : i + 1, :], x.shape)
+
+
+def factor_rows(panels):
+    panels = list(panels)
+    lane = lanes((8, 128))
+    row = lax.broadcasted_iota(jnp.int32, (8, 128), 0)
+    count = len(panels)
+    done = []
+    for k in range(count):
+        base = 8 * k
+        later = range(k + 1, count)
+        columns = [along_lanes(panels[k], base + j) for j in range(8)]
+        rows = [along_rows(panels[k], i) for i in range(8)]
+        below = {q: [along_lanes(panels[q], base + j) for j in range(8)] for q in later}
+        scaled = []
+        out = jnp.zeros((8, 128), F32)
+        for i in range(8):
+            pivot = along_rows(columns[i], i)
+            inverse = 1.0 / pivot
+            for j in range(i + 1, 8):
+                weight = along_rows(columns[j], i) * inverse
+                columns[j] = columns[j] - columns[i] * weight
+                rows[j] = rows[j] - rows[i] * weight
+                for q in later:
+                    below[q][j] = below[q][j] - below[q][i] * weight
+            scaled.append(rows[i] * inverse)
+            out = jnp.where(row == i, rows[i] * lax.rsqrt(pivot), out)
+        done.append(jnp.where(lane >= row + base, out, 0.0))
+        for q in later:
+            change = [below[q][i] * scaled[i] for i in range(8)]
+            while len(change) > 1:
+                change = [change[t] + change[t + 1] for t in range(0, len(change), 2)]
+            panels[q] = panels[q] - change[0]
+    return done
 
 
 def gram_kernel(whole_ref, gram_ref):
     cross = jnp.sum(whole_ref[:, 0:4, :], axis=0)
     lane = lanes((4, 128))
+    panels = []
     for a in range(16):
         low = jnp.zeros((4, 128), F32)
         high = jnp.zeros((4, 128), F32)
@@ -300,7 +343,14 @@
             high = jnp.where(inside, second, high)
         if a == 15:
             high = cross
-        gram_ref[8 * a : 8 * a + 8, :] = jnp.concatenate([low, high], axis=0)
+        panels.append(jnp.concatenate([low, high], axis=0))
+    turned = jnp.concatenate([panels[15]] * 16, axis=0).T
+    lane8 = lanes((8, 128))
+    for a in range(16):
+        rows = turned[8 * a : 8 * a + 8]
+        panels[a] = jnp.where(lane8 >= MODES, rows, panels[a])
+    for a, rows in enumerate(factor_rows(panels)):
+        gram_ref[8 * a : 8 * a + 8, :] = rows
 
 
 def gather_gram(whole):
@@ -308,6 +358,7 @@
         gram_kernel,
         out_shape=jax.ShapeDtypeStruct((COLS, 128), F32),
         name="gram",
+        compiler_params=pltpu.CompilerParams(vmem_limit_bytes=16 * 2**20),
     )(whole)
 
 
@@ -332,6 +383,7 @@
         owner_kernel,
         out_shape=jax.ShapeDtypeStruct((5, YPART, 256), F32),
         name="owner",
+        compiler_params=pltpu.CompilerParams(vmem_limit_bytes=16 * 2**20),
     )(back)
 
 
@@ -343,9 +395,8 @@
     whole, back = steps(w, recv, modes)
     whole = lax.all_to_all(whole, EVERYWHERE, split_axis=0, concat_axis=0, tiled=True)
     back = lax.all_to_all(back, "narrow", split_axis=0, concat_axis=0, tiled=True)
+    factor = gather_gram(whole)
     state = owner(back)[:, None]
-    gram = gather_gram(whole)
-    factor = jnp.linalg.cholesky(gram, symmetrize_input=False).T
     return (state, factor)
 
 

time: 87.1 us -> 70.7 us (0.81)
  other arithmetic: 13.9 us -> 0 us
  Pallas kernels: 17 us -> 14.1 us
  blocking collectives: 11.7 us -> 10.4 us
  local copies, waits for them, and re-layouts: 2.3 us -> 3.31 us
    another operation x3 -> x0, other arithmetic: 13.2 us -> none  [local(): factor = jnp.linalg.cholesky(gram, symmetrize_input=False).T]
    pallas_call x1, Pallas kernels: 1.97 us -> 5.08 us  [gather_gram(): pl.pallas_call(gram_kernel, out_shape=jax.ShapeDtypeStruct((COLS, 128), F...]
    pallas_call x1, Pallas kernels: 8.3 us -> 5.68 us  [steps(): pl.pallas_call(step_kernel, in_specs=[pl.BlockSpec(memory_space=pltpu.SME...]
    pallas_call x1, Pallas kernels: 5.14 us -> 2.63 us  [pack(): pl.pallas_call(pack_kernel, grid=(5,), in_specs=[pl.BlockSpec((5, YPART,...]
    all_to_all x1, blocking collectives: 11.7 us -> 10.4 us  [local(): lax.all_to_all(back, 'narrow', split_axis=0, concat_axis=0, tiled=True)]
    unnamed x5 -> x8, local copies, waits for them, and re-layouts: 2.3 us -> 3.31 us
  transfers between devices with their start and end apart: 2 -> 2, of which waited for: 2 -> 2; matrix products, arithmetic and copies ran while one was open for 0% -> 0% of each run, Pallas kernels for 2% -> 1%
where the time goes in v3:
time: 70.7 us; the launch traced here: 70.4 us
  waiting for transfers between devices  26 us (37%)
  starting transfers between devices  15.9 us (22%)
  Pallas kernels  14.1 us (20%)
  blocking collectives  10.4 us (15%)
  local copies, waits for them, and re-layouts  3.31 us (5%)
    all_to_all x1, waiting for transfers between devices, local(): lax.all_to_all(sent, EVERYWHERE, split_axis=0, concat_axis=0, tiled=True)  13.4 us
    all_to_all x1, waiting for transfers between devices, local(): lax.all_to_all(whole, EVERYWHERE, split_axis=0, concat_axis=0, tiled=True)  12.6 us
    all_to_all x1, starting transfers between devices, local(): lax.all_to_all(sent, EVERYWHERE, split_axis=0, concat_axis=0, tiled=True)  11.2 us
    all_to_all x1, blocking collectives, local(): lax.all_to_all(back, 'narrow', split_axis=0, concat_axis=0, tiled=True)  10.4 us
    pallas_call x1, Pallas kernels, steps(): pl.pallas_call(step_kernel, in_specs=[pl.BlockSpec(memory_space=pltpu.SME...  5.68 us
    pallas_call x1, Pallas kernels, gather_gram(): pl.pallas_call(gram_kernel, out_shape=jax.ShapeDtypeStruct((COLS, 128), F...  5.08 us
    all_to_all x1, starting transfers between devices, local(): lax.all_to_all(whole, EVERYWHERE, split_axis=0, concat_axis=0, tiled=True)  4.69 us
    unnamed x8, local copies, waits for them, and re-layouts  3.31 us
  transfers between devices with their start and end apart: 2, of which 2 were waited for; matrix products, arithmetic and copies ran while one was open for 0% of the time, Pallas kernels for 1%

profile of v3, /device:TPU:0, one launch (start us, length us, event | category | flops | bytes accessed | tf_op | source)
XLA Modules:
  0.0 70.4 jit_solution(17423117171181457778)
XLA Ops:
  0.6 0.0 copy-start
  0.6 1.7 %copy-done = bf16[124,5,1,2048]{3,0,2,1:T(8,128)(2,1)S(1)} copy-done((bf16[124,5,1,2048]{3,0,2,1:T(8,128)(2,1)S(1)}, bf16[124,5,1,2048]{3,0,2,1:T(8,128)(2,1)}, u32[]{:S(2)}) %copy-start) | copy-done | bytes 2539544
  2.4 0.0 copy-start.3
  2.4 0.8 %copy-done.3 = f32[5,1,8,256]{3,2,1,0:T(8,128)S(1)} copy-done((f32[5,1,8,256]{3,2,1,0:T(8,128)S(1)}, f32[5,1,8,256]{3,2,1,0:T(8,128)}, u32[]{:S(2)}) %copy-start.3) | copy-done | bytes 40984
  3.1 0.0 copy-start.1
  3.2 2.6 %pack.1 = bf16[16,8,16,128]{3,2,1,0:T(8,128)(2,1)} custom-call(f32[5,8,256]{2,1,0:T(8,128)S(1)} %bitcast.11, bf16[5,124,2048]{2,1,0:T(8,128)(2,1)S(1)} %bitcast.9), custom_call_target="tpu_custom_call" | custom-call | tf_op jit(solution)/shard_map/pack/pallas_call | solution.py:86
  5.8 11.2 %all-to-all-start = ((bf16[128,16,128]{2,1,0:T(8,128)(2,1)}), bf16[128,16,128]{2,1,0:T(8,128)(2,1)S(1)}, u32[]{:S(2)}, u32[]{:S(2)}) async-start(bf16[128,16,128]{2,1,0:T(8,128)(2,1)} %bitcast.4), calls=%async_computation | async-start | bytes 1048576 | tf_op jit(solution)/shard_map/all_to_all | solution.py:394
  17.0 13.4 %all-to-all-done.recv_ref = bf16[128,16,128]{2,1,0:T(8,128)(2,1)S(1)} async-done(((bf16[128,16,128]{2,1,0:T(8,128)(2,1)}), bf16[128,16,128]{2,1,0:T(8,128)(2,1)S(1)}, u32[]{:S(2)}, u32[]{:S(2)}) %all-to-all-start) | async-done | bytes 524320 | tf_op jit(solution)/shard_map/all_to_all | solution.py:394
  30.3 0.0 copy-done.1
  30.3 5.7 %steps.1 = (f32[128,8,128]{2,1,0:T(8,128)S(1)}, f32[8,16,128]{2,1,0:T(8,128)S(1)}) custom-call(s32[1]{0:T(128)} %bitcast.w_ref, bf16[128,16,128]{2,1,0:T(8,128)(2,1)S(1)} %all-to-all-done.recv_ref, bf16[5,124,2048]{2,1,0:T(8,128)(2,1)S(1)} %bitcast.10), custom_call_target="tpu_custom_call" | custom-call | tf_op jit(solution)/shard_map/steps/pallas_call | solution.py:261
  36.0 0.0 copy-start.2
  36.0 0.8 %copy-done.2 = f32[128,8,128]{2,1,0:T(8,128)} copy-done((f32[128,8,128]{2,1,0:T(8,128)}, f32[128,8,128]{2,1,0:T(8,128)S(1)}, u32[]{:S(2)}) %copy-start.2) | copy-done | bytes 524312
  36.8 10.4 %all_to_all.15.back_ref = f32[8,16,128]{2,1,0:T(8,128)S(1)} all-to-all(f32[8,16,128]{2,1,0:T(8,128)S(1)} %get-tuple-element.4), channel_id=1, replica_groups=mesh['wide'=16,'narrow'=8] {'narrow'}, dimensions={0} | all-to-all | bytes 131072 | tf_op jit(solution)/shard_map/all_to_all | solution.py:397
  47.2 4.7 %all-to-all-start.2 = ((f32[128,8,128]{2,1,0:T(8,128)}), f32[128,8,128]{2,1,0:T(8,128)S(1)}, u32[]{:S(2)}, u32[]{:S(2)}) async-start(f32[128,8,128]{2,1,0:T(8,128)} %copy-done.2), calls=%async_computation.2 | async-start | bytes 1048576 | tf_op jit(solution)/shard_map/all_to_all | solution.py:396
  51.9 0.7 %owner.1 = f32[5,8,256]{2,1,0:T(8,128)} custom-call(f32[8,16,128]{2,1,0:T(8,128)S(1)} %all_to_all.15.back_ref), custom_call_target="tpu_custom_call" | custom-call | tf_op jit(solution)/shard_map/owner/pallas_call | solution.py:382
  52.6 12.6 %all-to-all-done.2.whole_ref = f32[128,8,128]{2,1,0:T(8,128)S(1)} async-done(((f32[128,8,128]{2,1,0:T(8,128)}), f32[128,8,128]{2,1,0:T(8,128)S(1)}, u32[]{:S(2)}, u32[]{:S(2)}) %all-to-all-start.2) | async-done | bytes 524320 | tf_op jit(solution)/shard_map/all_to_all | solution.py:396
  65.3 5.1 %gram.1 = f32[128,128]{1,0:T(8,128)} custom-call(f32[128,8,128]{2,1,0:T(8,128)S(1)} %all-to-all-done.2.whole_ref), custom_call_target="tpu_custom_call" | custom-call | tf_op jit(solution)/shard_map/gram/pallas_call | solution.py:357
Async XLA Ops:
  0.6 1.7 %copy-start = (bf16[124,5,1,2048]{3,0,2,1:T(8,128)(2,1)S(1)}, bf16[124,5,1,2048]{3,0,2,1:T(8,128)(2,1)}, u32[]{:S(2)}) copy-start(bf16[124,5,1,2048]{3,0,2,1:T(8,128)(2,1)} %param.3) | copy-start | bytes 7618564
  2.4 0.8 %copy-start.3 = (f32[5,1,8,256]{3,2,1,0:T(8,128)S(1)}, f32[5,1,8,256]{3,2,1,0:T(8,128)}, u32[]{:S(2)}) copy-start(f32[5,1,8,256]{3,2,1,0:T(8,128)} %param.2) | copy-start | bytes 122884
  3.1 27.2 %copy-start.1 = (bf16[124,5,1,2048]{3,0,2,1:T(8,128)(2,1)S(1)}, bf16[124,5,1,2048]{3,0,2,1:T(8,128)(2,1)}, u32[]{:S(2)}) copy-start(bf16[124,5,1,2048]{3,0,2,1:T(8,128)(2,1)} %param.3) | copy-start | bytes 7618564
  5.8 24.6 %all-to-all-start = ((bf16[128,16,128]{2,1,0:T(8,128)(2,1)}), bf16[128,16,128]{2,1,0:T(8,128)(2,1)S(1)}, u32[]{:S(2)}, u32[]{:S(2)}) async-start(bf16[128,16,128]{2,1,0:T(8,128)(2,1)} %bitcast.4), calls=%async_computation | async-start | bytes 1048576 | tf_op jit(solution)/shard_map/all_to_all | solution.py:394
  36.0 0.8 %copy-start.2 = (f32[128,8,128]{2,1,0:T(8,128)}, f32[128,8,128]{2,1,0:T(8,128)S(1)}, u32[]{:S(2)}) copy-start(f32[128,8,128]{2,1,0:T(8,128)S(1)} %get-tuple-element.5) | copy-start | bytes 1572868
  47.2 18.1 %all-to-all-start.2 = ((f32[128,8,128]{2,1,0:T(8,128)}), f32[128,8,128]{2,1,0:T(8,128)S(1)}, u32[]{:S(2)}, u32[]{:S(2)}) async-start(f32[128,8,128]{2,1,0:T(8,128)} %copy-done.2), calls=%async_computation.2 | async-start | bytes 1048576 | tf_op jit(solution)/shard_map/all_to_all | solution.py:396

commit v4 on v3

v4 whole, which is shorter than its diff:
```python
import functools

import jax
import jax.numpy as jnp
from jax import lax
from jax.experimental import pallas as pl
from jax.experimental.pallas import tpu as pltpu
from jax.sharding import PartitionSpec as P

GAMMA = 1.4
TIME_STEP = 0.25
VISCOSITY = 0.15
HALO = 4
WIDE = 16
NARROW = 8
DEVICES = WIDE * NARROW
MODES = 124
COLS = 128
ZPART = 32
WINDOW = ZPART + 2 * HALO
YPART = 8
NY = 64
INVERSE_CELLS = 1.0 / 262144.0
EVERYWHERE = ("wide", "narrow")
F32 = jnp.float32
BF16 = jnp.bfloat16


def lanes(shape):
    return lax.broadcasted_iota(jnp.int32, shape, len(shape) - 1)


def pack_kernel(fields_hbm, modes_hbm, out_hbm, modes_ref, known_ref, fields_ref, out_ref, sem):
    copies = [
        pltpu.make_async_copy(modes_hbm.at[c], modes_ref.at[c], sem.at[c]) for c in range(5)
    ]
    own = pltpu.make_async_copy(fields_hbm, fields_ref, sem.at[5])
    own.start()
    for copy in copies:
        copy.start()
    own.wait()
    lane = lanes((YPART, 128))
    lane_full = lanes((COLS, 128))
    means = []
    shifted = []
    for c in range(5):
        field = fields_ref[c]
        total = jnp.sum(jnp.sum(field, axis=0, keepdims=True), axis=1, keepdims=True)
        mean = (total * (1.0 / (YPART * 256))).astype(BF16).astype(F32)
        rounded = (field - mean).astype(BF16).astype(F32)
        known_ref[c] = rounded + mean
        means.append(jnp.broadcast_to(mean, (YPART, 128)))
        shifted.append(rounded)
    tail = jnp.zeros((YPART, 128), F32)
    for c in range(5):
        tail = jnp.where(lane == 3 * WINDOW + c, means[c], tail)
    halves = []
    for n in range(NARROW):
        def window(c, place):
            amount = (place * WINDOW + HALO - ZPART * n) % 256
            moved = pltpu.roll(shifted[c], amount, 1) if amount else shifted[c]
            return moved[:, 0:128]

        first = jnp.where(
            lane < WINDOW,
            window(0, 0),
            jnp.where(lane < 2 * WINDOW, window(1, 1), window(2, 2)),
        )
        first = jnp.where(lane < 3 * WINDOW, first, tail)
        second = jnp.where(lane < WINDOW, window(3, 0), window(4, 1))
        halves.append((first, second))

    gram = jnp.zeros((MODES, MODES), F32)
    for c in range(5):
        copies[c].wait()
        block = modes_ref[c]
        gram += lax.dot_general(
            block, block, (((1,), (1,)), ((), ())), preferred_element_type=F32
        )
    gram = jnp.concatenate([gram, jnp.zeros((MODES, COLS - MODES), F32)], axis=1)
    gram = jnp.concatenate([gram, jnp.zeros((COLS - MODES, 128), F32)], axis=0)
    high = gram.astype(BF16).astype(F32)
    rest = gram - high
    middle = rest.astype(BF16).astype(F32)
    low = rest - middle
    sends = []
    for n in range(NARROW):
        def turned(x, place):
            amount = (place - 16 * n) % 128
            return pltpu.roll(x, amount, 1) if amount else x

        first, second = halves[n]
        parts = jnp.where(
            lane_full < 96,
            turned(high, 80),
            jnp.where(lane_full < 112, turned(middle, 96), turned(low, 112)),
        ).reshape(WIDE, YPART, 128)
        lower = jnp.broadcast_to(first[None], (WIDE, YPART, 128))
        upper = jnp.where(lane[None] < 2 * WINDOW, second[None], parts)
        out_ref[:, n] = jnp.concatenate([lower, upper], axis=1).astype(BF16)
        send = pltpu.make_async_copy(out_ref.at[:, n], out_hbm.at[:, n], sem.at[6 + n])
        send.start()
        sends.append(send)
    for send in sends:
        send.wait()


def pack(fields, modes):
    return pl.pallas_call(
        pack_kernel,
        in_specs=[
            pl.BlockSpec(memory_space=pltpu.HBM),
            pl.BlockSpec(memory_space=pltpu.HBM),
        ],
        out_specs=[
            pl.BlockSpec(memory_space=pltpu.HBM),
            pl.BlockSpec(memory_space=pltpu.VMEM),
            pl.BlockSpec(memory_space=pltpu.VMEM),
        ],
        out_shape=[
            pltpu.HBM((WIDE, NARROW, 16, 128), BF16),
            jax.ShapeDtypeStruct((5, MODES, 2048), BF16),
            jax.ShapeDtypeStruct((5, YPART, 256), F32),
        ],
        scratch_shapes=[
            pltpu.VMEM((5, YPART, 256), F32),
            pltpu.VMEM((WIDE, NARROW, 16, 128), BF16),
            pltpu.SemaphoreType.DMA((6 + NARROW,)),
        ],
        name="pack",
        compiler_params=pltpu.CompilerParams(vmem_limit_bytes=16 * 2**20),
    )(
        pltpu.with_memory_space_constraint(fields, pltpu.HBM),
        pltpu.with_memory_space_constraint(modes, pltpu.HBM),
    )


def up(x, axis):
    return pltpu.roll(x, x.shape[axis] - 1, axis)


def down(x, axis):
    return pltpu.roll(x, 1, axis)


def fluxes(u, directions):
    density, m1, m2, m3, energy = u
    half = 0.5 * TIME_STEP
    share = half / density
    momenta = (m1, m2, m3)
    v = [m * share for m in momenta]
    products = {(i, i): momenta[i] * v[i] for i in range(3)}
    squares = products[(0, 0)] + products[(1, 1)] + products[(2, 2)]
    pressure = (half * (GAMMA - 1.0)) * energy - (0.5 * (GAMMA - 1.0)) * squares
    total = energy + (1.0 / half) * pressure
    out = []
    for d in directions:
        row = [half * momenta[d]]
        for i in range(3):
            if i == d:
                row.append(products[(d, d)] + pressure)
            else:
                key = (min(i, d), max(i, d))
                if key not in products:
                    products[key] = momenta[key[0]] * v[key[1]]
                row.append(products[key])
        row.append(total * v[d])
        out.append(row)
    return out


CENTRE = 1.0 - 6.0 * VISCOSITY * TIME_STEP
SOFT = VISCOSITY * TIME_STEP


def across(u):
    flux = fluxes(u, (0,))[0]
    smooth = [SOFT * x for x in u]
    ahead = [smooth[c] - flux[c] for c in range(5)]
    behind = [smooth[c] + flux[c] for c in range(5)]
    return ahead, behind


def within(u):
    rows = fluxes(u, (0, 1, 2))
    smooth = [SOFT * x for x in u]
    ahead = [smooth[c] - rows[0][c] for c in range(5)]
    behind = [smooth[c] + rows[0][c] for c in range(5)]
    total = []
    for c in range(5):
        total.append(
            CENTRE * u[c]
            + (up(smooth[c] - rows[1][c], 0) + down(smooth[c] + rows[1][c], 0))
            + (up(smooth[c] - rows[2][c], 1) + down(smooth[c] + rows[2][c], 1))
        )
    return ahead, behind, total


def joined(total, ahead, behind, after, before, lane):
    out = []
    for c in range(5):
        plus = pltpu.roll(ahead[c], 128 - WINDOW, 1)
        if after is not None:
            plus = jnp.where(lane < 2 * WINDOW, plus, pltpu.roll(after[c], 2 * WINDOW, 1))
        minus = pltpu.roll(behind[c], WINDOW, 1)
        if before is not None:
            minus = jnp.where(lane < WINDOW, pltpu.roll(before[c], 128 - 2 * WINDOW, 1), minus)
        out.append(total[c] + (plus + minus))
    return out


def section_all(load, lane):
    parts = []
    for g in range(3):
        parts.append(within(load(g)))
        if g >= 1:
            ahead, behind, total = parts[g - 1]
            before = parts[g - 2][1] if g >= 2 else None
            yield g - 1, joined(total, ahead, behind, parts[g][0], before, lane)
    ahead, behind, total = parts[2]
    yield 2, joined(total, ahead, behind, None, parts[1][1], lane)


def step_kernel(w_ref, recv_ref, modes_ref, whole_ref, base, one, two, turn_ref):
    w = w_ref[0]
    lane = lanes((NY, 128))

    for g in range(3):
        planes = []
        places = []
        for j in range(3):
            start = lax.rem(w + (3 * g - 4 + j + WIDE), WIDE) * NARROW
            block = recv_ref[pl.ds(start, NARROW)].astype(F32)
            planes.append((block[:, 0:8].reshape(NY, 128), block[:, 8:16].reshape(NY, 128)))
            places.append((lane >= WINDOW * j) & (lane < WINDOW * (j + 1)))
        for c in range(5):
            moved = []
            for j in range(3):
                amount = WINDOW * (j - c % 3) % 128
                value = planes[j][c // 3]
                moved.append(pltpu.roll(value, amount, 1) if amount else value)
            value = jnp.where(places[0], moved[0], jnp.where(places[1], moved[1], moved[2]))
            at = 3 * WINDOW + c
            mean = [
                jnp.broadcast_to(planes[j][0][:, at : at + 1], (NY, 128)) for j in range(3)
            ]
            mean = jnp.where(places[0], mean[0], jnp.where(places[1], mean[1], mean[2]))
            base[g, c] = value + mean

    terms = recv_ref[:, 8:16, :].astype(F32)
    summed = jnp.sum(terms, axis=0)
    block = (pltpu.roll(summed, 16, 1) + pltpu.roll(summed, 32, 1)) + pltpu.roll(summed, 48, 1)

    packed = [jnp.zeros((NY, 128), F32) for _ in range(5)]

    def keep(index, u, out):
        for c in range(5):
            value = pltpu.roll(u[c], (ZPART * index - WINDOW - HALO) % 128, 1)
            inside = (lane >= ZPART * index) & (lane < ZPART * (index + 1))
            out[c] = jnp.where(inside, value, out[c])

    def stored(ref):
        return lambda g: [ref[g, c] for c in range(5)]

    for g, v in section_all(stored(base), lane):
        for c in range(5):
            one[g, c] = v[c]
        if g == 1:
            keep(0, v, packed)
    for g, v in section_all(stored(one), lane):
        new = [0.5 * (base[g, c] + v[c]) for c in range(5)]
        for c in range(5):
            two[g, c] = new[c]
        if g == 1:
            keep(1, new, packed)
    outer = [jnp.where(lane < WINDOW, two[2, c], two[0, c]) for c in range(5)]
    after, before = across(outer)
    ahead, behind, total = within([two[1, c] for c in range(5)])
    third = joined(total, ahead, behind, after, before, lane)
    keep(2, third, packed)
    ahead, behind, total = within(third)
    fourth = joined(total, ahead, behind, None, None, lane)
    fourth = [0.5 * (two[1, c] + fourth[c]) for c in range(5)]
    keep(3, fourth, packed)
    change = [fourth[c] - base[1, c] for c in range(5)]
    spread = jnp.zeros((NY, 128), F32)
    for c in range(4):
        value = pltpu.roll(change[c], (ZPART * c - WINDOW - HALO) % 128, 1)
        inside = (lane >= ZPART * c) & (lane < ZPART * (c + 1))
        spread = jnp.where(inside, value, spread)
    last = pltpu.roll(change[4], 128 - WINDOW - HALO, 1)

    cross = jnp.zeros((4, MODES), F32)
    square = jnp.zeros((4, 4), F32)
    contract = (((1,), (1,)), ((), ()))
    for c in range(5):
        rounded = packed[c].astype(BF16).astype(F32)
        pair = jnp.concatenate([rounded, pltpu.roll(rounded, 127, 1)], axis=0)
        turn_ref[c] = pair.T
    for c in range(5):
        chunks = [turn_ref[c, pl.ds(2 * k, 4, stride=ZPART), :] for k in range(16)]
        rows = jnp.concatenate(chunks, axis=1).astype(BF16)
        cross += lax.dot_general(rows, modes_ref[c], contract, preferred_element_type=F32)
        square += lax.dot_general(rows, rows, contract, preferred_element_type=F32)
    top = jnp.concatenate([cross, square], axis=1) * INVERSE_CELLS
    high = top.astype(BF16).astype(F32)
    first = jnp.concatenate([high, top - high], axis=0)
    lane8 = lanes((8, 128))
    block = block * INVERSE_CELLS
    high = block.astype(BF16).astype(F32)
    rest = block - high
    middle = rest.astype(BF16).astype(F32)
    addends = jnp.where(
        lane8 < 48,
        pltpu.roll(high, 32, 1),
        jnp.where(lane8 < 64, pltpu.roll(middle, 48, 1), pltpu.roll(rest - middle, 64, 1)),
    )
    for n in range(NARROW):
        rows = slice(YPART * n, YPART * (n + 1))
        third_rows = jnp.where(lane8 < ZPART, last[rows], jnp.where(lane8 < 80, addends, 0.0))
        piece = jnp.concatenate([first, spread[rows], third_rows], axis=0).astype(BF16)
        whole_ref[:, n] = jnp.broadcast_to(piece[None], (WIDE, 24, 128))


def steps(w, recv, modes):
    return pl.pallas_call(
        step_kernel,
        in_specs=[
            pl.BlockSpec(memory_space=pltpu.SMEM),
            pl.BlockSpec(memory_space=pltpu.VMEM),
            pl.BlockSpec(memory_space=pltpu.VMEM),
        ],
        out_specs=pl.BlockSpec(memory_space=pltpu.VMEM),
        out_shape=jax.ShapeDtypeStruct((WIDE, NARROW, 24, 128), BF16),
        scratch_shapes=[
            pltpu.VMEM((3, 5, NY, 128), F32),
            pltpu.VMEM((3, 5, NY, 128), F32),
            pltpu.VMEM((3, 5, NY, 128), F32),
            pltpu.VMEM((5, 128, 128), F32),
        ],
        name="steps",
        compiler_params=pltpu.CompilerParams(vmem_limit_bytes=24 * 2**20),
    )(w, recv, modes)


def along_lanes(x, j):
    return jnp.broadcast_to(x[:, j : j + 1], x.shape)


def along_rows(x, i):
    return jnp.broadcast_to(x[i : i + 1, :], x.shape)


def factor_rows(panels):
    panels = list(panels)
    lane = lanes((8, 128))
    row = lax.broadcasted_iota(jnp.int32, (8, 128), 0)
    count = len(panels)
    done = []
    for k in range(count):
        base = 8 * k
        later = range(k + 1, count)
        columns = [along_lanes(panels[k], base + j) for j in range(8)]
        rows = [along_rows(panels[k], i) for i in range(8)]
        below = {q: [along_lanes(panels[q], base + j) for j in range(8)] for q in later}
        scaled = []
        out = jnp.zeros((8, 128), F32)
        for i in range(8):
            pivot = along_rows(columns[i], i)
            inverse = 1.0 / pivot
            for j in range(i + 1, 8):
                weight = along_rows(columns[j], i) * inverse
                columns[j] = columns[j] - columns[i] * weight
                rows[j] = rows[j] - rows[i] * weight
                for q in later:
                    below[q][j] = below[q][j] - below[q][i] * weight
            scaled.append(rows[i] * inverse)
            out = jnp.where(row == i, rows[i] * lax.rsqrt(pivot), out)
        done.append(jnp.where(lane >= row + base, out, 0.0))
        for q in later:
            change = [below[q][i] * scaled[i] for i in range(8)]
            while len(change) > 1:
                change = [change[t] + change[t + 1] for t in range(0, len(change), 2)]
            panels[q] = panels[q] - change[0]
    return done


def finish_kernel(w_ref, whole_ref, known_ref, factor_ref, state_ref):
    sums = jnp.sum(whole_ref[:, 0:8, :].astype(F32), axis=0)
    cross = sums[0:4] + sums[4:8]
    lane8 = lanes((8, 128))
    source = lax.broadcasted_iota(jnp.int32, (COLS, 128), 0)
    target = lanes((COLS, 128))
    gram = jnp.zeros((COLS, 128), F32)
    every = whole_ref[...].reshape(WIDE, NARROW, 24, 128)[:, :, 16:24, :].astype(F32)
    for b in range(8):
        held = (source >= ZPART) & (source < ZPART + 48) & (target >= 16 * b)
        chosen = jnp.where(held & (target == 16 * b + source % 16), 1.0, 0.0).astype(BF16)
        rows = every[:, b].reshape(COLS, 128).astype(BF16)
        gram += jnp.dot(rows, chosen, preferred_element_type=F32)
    panels = [gram[8 * a : 8 * a + 8] for a in range(16)]
    panels[15] = jnp.concatenate([panels[15][0:4], cross], axis=0)
    turned = jnp.concatenate([panels[15]] * 16, axis=0).T
    for a in range(16):
        panels[a] = jnp.where(lane8 >= MODES, turned[8 * a : 8 * a + 8], panels[a])
    for a, rows in enumerate(factor_rows(panels)):
        factor_ref[8 * a : 8 * a + 8, :] = rows

    home = whole_ref[pl.ds(w_ref[0] * NARROW, NARROW), 8:24, :].astype(F32)
    lane = lanes((YPART, 256))
    for c in range(5):
        total = jnp.zeros((YPART, 256), F32)
        place = ZPART * (c % 4)
        row = 8 * (c // 4)
        for n in range(NARROW):
            part = home[n, row : row + 8, :]
            part = jnp.concatenate([part, part], axis=1)
            amount = (ZPART * n - place) % 256
            part = pltpu.roll(part, amount, 1) if amount else part
            inside = (lane >= ZPART * n) & (lane < ZPART * (n + 1))
            total = jnp.where(inside, part, total)
        state_ref[c] = known_ref[c] + total


def finish(w, whole, known):
    return pl.pallas_call(
        finish_kernel,
        in_specs=[
            pl.BlockSpec(memory_space=pltpu.SMEM),
            pl.BlockSpec(memory_space=pltpu.VMEM),
            pl.BlockSpec(memory_space=pltpu.VMEM),
        ],
        out_shape=[
            jax.ShapeDtypeStruct((COLS, 128), F32),
            jax.ShapeDtypeStruct((5, YPART, 256), F32),
        ],
        name="finish",
        compiler_params=pltpu.CompilerParams(vmem_limit_bytes=16 * 2**20),
    )(w, whole, known)


def local(fields, prior_modes):
    modes = jnp.transpose(prior_modes[:, :, 0, :], (1, 0, 2))
    w = lax.axis_index("wide").astype(jnp.int32).reshape(1)
    sent, modes, known = pack(fields[:, 0], modes)
    sent = sent.reshape(DEVICES, 16, 128)
    recv = lax.all_to_all(sent, EVERYWHERE, split_axis=0, concat_axis=0, tiled=True)
    whole = steps(w, recv, modes).reshape(DEVICES, 24, 128)
    whole = lax.all_to_all(whole, EVERYWHERE, split_axis=0, concat_axis=0, tiled=True)
    factor, state = finish(w, whole, known)
    return (state[:, None], factor)


def solution(mesh):
    placed = (P(None, "wide", "narrow", None), P(None, None, "wide", "narrow"))
    return jax.shard_map(
        local,
        mesh=mesh,
        in_specs=placed,
        out_specs=(P(None, "wide", "narrow", None), P()),
        check_vma=False,
    )
```

time: 70.7 us -> 58.6 us (0.83)
  waiting for transfers between devices: 26 us -> 13.4 us
  blocking collectives: 10.4 us -> 20.4 us
  starting transfers between devices: 15.9 us -> 11.2 us
  local copies, waits for them, and re-layouts: 3.31 us -> 0 us
  Pallas kernels: 14.1 us -> 12.8 us
    all_to_all x1 -> x0, waiting for transfers between devices: 12.6 us -> none  [local(): lax.all_to_all(whole, EVERYWHERE, split_axis=0, concat_axis=0, tiled=True)]
    all_to_all x1, blocking collectives: 10.4 us -> 20.4 us  [local(): lax.all_to_all(whole, EVERYWHERE, split_axis=0, concat_axis=0, tiled=True)]
    all_to_all x1 -> x0, starting transfers between devices: 4.69 us -> none  [local(): lax.all_to_all(whole, EVERYWHERE, split_axis=0, concat_axis=0, tiled=True)]
    unnamed x8 -> x0, local copies, waits for them, and re-layouts: 3.31 us -> none
    pallas_call x1, Pallas kernels: 5.68 us -> 3.91 us  [steps(): pl.pallas_call(step_kernel, in_specs=[pl.BlockSpec(memory_space=pltpu.SME...]
    pallas_call x3 -> x2, Pallas kernels: 8.43 us -> 8.93 us  [the longest x1 4.96 us: finish(): pl.pallas_call(finish_kernel, in_specs=[pl.BlockSpec(memory_space=pltpu.S...]
  transfers between devices with their start and end apart: 2 -> 1, of which waited for: 2 -> 1; matrix products, arithmetic and copies ran while one was open for 0% -> 0% of each run, Pallas kernels for 1% -> 0%
where the time goes in v4:
time: 58.6 us; the launch traced here: 58.4 us
  blocking collectives  20.4 us (35%)
  waiting for transfers between devices  13.4 us (23%)
  Pallas kernels  12.8 us (22%)
  starting transfers between devices  11.2 us (19%)
  between operations  0.66 us (1%)
    all_to_all x1, blocking collectives, local(): lax.all_to_all(whole, EVERYWHERE, split_axis=0, concat_axis=0, tiled=True)  20.4 us
    all_to_all x1, waiting for transfers between devices, local(): lax.all_to_all(sent, EVERYWHERE, split_axis=0, concat_axis=0, tiled=True)  13.4 us
    all_to_all x1, starting transfers between devices, local(): lax.all_to_all(sent, EVERYWHERE, split_axis=0, concat_axis=0, tiled=True)  11.2 us
    pallas_call x1, Pallas kernels, finish(): pl.pallas_call(finish_kernel, in_specs=[pl.BlockSpec(memory_space=pltpu.S...  4.96 us
    pallas_call x1, Pallas kernels, pack(): pl.pallas_call(pack_kernel, in_specs=[pl.BlockSpec(memory_space=pltpu.HBM...  3.97 us
    pallas_call x1, Pallas kernels, steps(): pl.pallas_call(step_kernel, in_specs=[pl.BlockSpec(memory_space=pltpu.SME...  3.91 us
  transfers between devices with their start and end apart: 1, of which 1 were waited for; matrix products, arithmetic and copies ran while one was open for 0% of the time, Pallas kernels for 0%

profile of v4, /device:TPU:0, one launch (start us, length us, event | category | flops | bytes accessed | tf_op | source)
XLA Modules:
  0.0 58.4 jit_solution(6824627168690730037)
XLA Ops:
  0.6 4.0 %pack.1 = (bf16[16,8,16,128]{3,2,1,0:T(8,128)(2,1)}, bf16[5,124,2048]{2,1,0:T(8,128)(2,1)S(1)}, f32[5,8,256]{2,1,0:T(8,128)S(1)}) custom-call(f32[5,8,256]{2,1,0:T(8,128)} %bitcast.13, bf16[5,124,2048]{2,1,0:T(8,128)(2,1)} %bitcast.11), custom_call_target="tpu_custom_call" | custom-call | tf_op jit(solution)/shard_map/pack/pallas_call | solution.py:109
  4.6 11.2 %all-to-all-start = ((bf16[128,16,128]{2,1,0:T(8,128)(2,1)}), bf16[128,16,128]{2,1,0:T(8,128)(2,1)S(1)}, u32[]{:S(2)}, u32[]{:S(2)}) async-start(bf16[128,16,128]{2,1,0:T(8,128)(2,1)} %bitcast.12), calls=%async_computation | async-start | bytes 1048576 | tf_op jit(solution)/shard_map/all_to_all | solution.py:447
  15.8 13.4 %all-to-all-done.recv_ref = bf16[128,16,128]{2,1,0:T(8,128)(2,1)S(1)} async-done(((bf16[128,16,128]{2,1,0:T(8,128)(2,1)}), bf16[128,16,128]{2,1,0:T(8,128)(2,1)S(1)}, u32[]{:S(2)}, u32[]{:S(2)}) %all-to-all-start) | async-done | bytes 524320 | tf_op jit(solution)/shard_map/all_to_all | solution.py:447
  29.2 3.9 %steps.1 = bf16[16,8,24,128]{3,2,1,0:T(8,128)(2,1)S(1)} custom-call(s32[1]{0:T(128)} %bitcast.w_ref, bf16[128,16,128]{2,1,0:T(8,128)(2,1)S(1)} %all-to-all-done.recv_ref, bf16[5,124,2048]{2,1,0:T(8,128)(2,1)S(1)} %get-tuple-element.8.modes_ref), custom_call_target="tpu_custom_call" | custom-call | tf_op jit(solution)/shard_map/steps/pallas_call | solution.py:326
  33.1 20.4 %all_to_all.10.whole_ref = bf16[128,24,128]{2,1,0:T(8,128)(2,1)S(1)} all-to-all(bf16[128,24,128]{2,1,0:T(8,128)(2,1)S(1)} %bitcast.10), channel_id=1, replica_groups=mesh['wide'=16,'narrow'=8] {'wide','narrow'}, dimensions={0} | all-to-all | bytes 1572864 | tf_op jit(solution)/shard_map/all_to_all | solution.py:449
  53.5 5.0 %finish.1 = (f32[128,128]{1,0:T(8,128)}, f32[5,8,256]{2,1,0:T(8,128)}) custom-call(s32[1]{0:T(128)} %bitcast.w_ref, bf16[128,24,128]{2,1,0:T(8,128)(2,1)S(1)} %all_to_all.10.whole_ref, f32[5,8,256]{2,1,0:T(8,128)S(1)} %get-tuple-element.9.known_ref), custom_call_target="tpu_custom_call" | custom-call | tf_op jit(solution)/shard_map/finish/pallas_call | solution.py:426
Async XLA Ops:
  4.6 24.5 %all-to-all-start = ((bf16[128,16,128]{2,1,0:T(8,128)(2,1)}), bf16[128,16,128]{2,1,0:T(8,128)(2,1)S(1)}, u32[]{:S(2)}, u32[]{:S(2)}) async-start(bf16[128,16,128]{2,1,0:T(8,128)(2,1)} %bitcast.12), calls=%async_computation | async-start | bytes 1048576 | tf_op jit(solution)/shard_map/all_to_all | solution.py:447

commit v5 on v4

--- a/solution.py
+++ b/solution.py
@@ -14,6 +14,7 @@
 WIDE = 16
 NARROW = 8
 DEVICES = WIDE * NARROW
+CHIPS = WIDE // 2
 MODES = 124
 COLS = 128
 ZPART = 32
@@ -30,7 +31,7 @@
     return lax.broadcasted_iota(jnp.int32, shape, len(shape) - 1)
 
 
-def pack_kernel(fields_hbm, modes_hbm, out_hbm, modes_ref, known_ref, fields_ref, out_ref, sem):
+def pack_kernel(fields_hbm, modes_hbm, out_ref, modes_ref, known_ref, fields_ref, sem):
     copies = [
         pltpu.make_async_copy(modes_hbm.at[c], modes_ref.at[c], sem.at[c]) for c in range(5)
     ]
@@ -83,7 +84,6 @@
     rest = gram - high
     middle = rest.astype(BF16).astype(F32)
     low = rest - middle
-    sends = []
     for n in range(NARROW):
         def turned(x, place):
             amount = (place - 16 * n) % 128
@@ -98,11 +98,6 @@
         lower = jnp.broadcast_to(first[None], (WIDE, YPART, 128))
         upper = jnp.where(lane[None] < 2 * WINDOW, second[None], parts)
         out_ref[:, n] = jnp.concatenate([lower, upper], axis=1).astype(BF16)
-        send = pltpu.make_async_copy(out_ref.at[:, n], out_hbm.at[:, n], sem.at[6 + n])
-        send.start()
-        sends.append(send)
-    for send in sends:
-        send.wait()
 
 
 def pack(fields, modes):
@@ -113,19 +108,18 @@
             pl.BlockSpec(memory_space=pltpu.HBM),
         ],
         out_specs=[
-            pl.BlockSpec(memory_space=pltpu.HBM),
+            pl.BlockSpec(memory_space=pltpu.VMEM),
             pl.BlockSpec(memory_space=pltpu.VMEM),
             pl.BlockSpec(memory_space=pltpu.VMEM),
         ],
         out_shape=[
-            pltpu.HBM((WIDE, NARROW, 16, 128), BF16),
+            jax.ShapeDtypeStruct((WIDE, NARROW, 16, 128), BF16),
             jax.ShapeDtypeStruct((5, MODES, 2048), BF16),
             jax.ShapeDtypeStruct((5, YPART, 256), F32),
         ],
         scratch_shapes=[
             pltpu.VMEM((5, YPART, 256), F32),
-            pltpu.VMEM((WIDE, NARROW, 16, 128), BF16),
-            pltpu.SemaphoreType.DMA((6 + NARROW,)),
+            pltpu.SemaphoreType.DMA((6,)),
         ],
         name="pack",
         compiler_params=pltpu.CompilerParams(vmem_limit_bytes=16 * 2**20),
@@ -181,7 +175,15 @@
     return ahead, behind
 
 
-def within(u):
+def beside(above, below, edge, slot):
+    edge[0, slot, 8 : 8 + NY] = above
+    edge[0, slot, 8 + NY : 9 + NY] = above[0:1]
+    edge[1, slot, 8 : 8 + NY] = below
+    edge[1, slot, 7:8] = below[NY - 1 : NY]
+    return edge[0, slot, 9 : 9 + NY] + edge[1, slot, 7 : 7 + NY]
+
+
+def within(u, edge, slot):
     rows = fluxes(u, (0, 1, 2))
     smooth = [SOFT * x for x in u]
     ahead = [smooth[c] - rows[0][c] for c in range(5)]
@@ -190,7 +192,7 @@
     for c in range(5):
         total.append(
             CENTRE * u[c]
-            + (up(smooth[c] - rows[1][c], 0) + down(smooth[c] + rows[1][c], 0))
+            + beside(smooth[c] - rows[1][c], smooth[c] + rows[1][c], edge, 5 * slot + c)
             + (up(smooth[c] - rows[2][c], 1) + down(smooth[c] + rows[2][c], 1))
         )
     return ahead, behind, total
@@ -209,10 +211,10 @@
     return out
 
 
-def section_all(load, lane):
+def section_all(load, lane, edge, slot):
     parts = []
     for g in range(3):
-        parts.append(within(load(g)))
+        parts.append(within(load(g), edge, slot + g))
         if g >= 1:
             ahead, behind, total = parts[g - 1]
             before = parts[g - 2][1] if g >= 2 else None
@@ -221,7 +223,7 @@
     yield 2, joined(total, ahead, behind, None, parts[1][1], lane)
 
 
-def step_kernel(w_ref, recv_ref, modes_ref, whole_ref, base, one, two, turn_ref):
+def step_kernel(w_ref, recv_ref, modes_ref, pair_ref, home_ref, base, one, two, turn_ref, edge):
     w = w_ref[0]
     lane = lanes((NY, 128))
 
@@ -262,12 +264,12 @@
     def stored(ref):
         return lambda g: [ref[g, c] for c in range(5)]
 
-    for g, v in section_all(stored(base), lane):
+    for g, v in section_all(stored(base), lane, edge, 0):
         for c in range(5):
             one[g, c] = v[c]
         if g == 1:
             keep(0, v, packed)
-    for g, v in section_all(stored(one), lane):
+    for g, v in section_all(stored(one), lane, edge, 3):
         new = [0.5 * (base[g, c] + v[c]) for c in range(5)]
         for c in range(5):
             two[g, c] = new[c]
@@ -275,10 +277,10 @@
             keep(1, new, packed)
     outer = [jnp.where(lane < WINDOW, two[2, c], two[0, c]) for c in range(5)]
     after, before = across(outer)
-    ahead, behind, total = within([two[1, c] for c in range(5)])
+    ahead, behind, total = within([two[1, c] for c in range(5)], edge, 6)
     third = joined(total, ahead, behind, after, before, lane)
     keep(2, third, packed)
-    ahead, behind, total = within(third)
+    ahead, behind, total = within(third, edge, 7)
     fourth = joined(total, ahead, behind, None, None, lane)
     fourth = [0.5 * (two[1, c] + fourth[c]) for c in range(5)]
     keep(3, fourth, packed)
@@ -288,7 +290,8 @@
         value = pltpu.roll(change[c], (ZPART * c - WINDOW - HALO) % 128, 1)
         inside = (lane >= ZPART * c) & (lane < ZPART * (c + 1))
         spread = jnp.where(inside, value, spread)
-    last = pltpu.roll(change[4], 128 - WINDOW - HALO, 1)
+    home_ref[0] = spread
+    home_ref[1] = pltpu.roll(change[4], 128 - WINDOW - HALO, 1)
 
     cross = jnp.zeros((4, MODES), F32)
     square = jnp.zeros((4, 4), F32)
@@ -303,8 +306,6 @@
         cross += lax.dot_general(rows, modes_ref[c], contract, preferred_element_type=F32)
         square += lax.dot_general(rows, rows, contract, preferred_element_type=F32)
     top = jnp.concatenate([cross, square], axis=1) * INVERSE_CELLS
-    high = top.astype(BF16).astype(F32)
-    first = jnp.concatenate([high, top - high], axis=0)
     lane8 = lanes((8, 128))
     block = block * INVERSE_CELLS
     high = block.astype(BF16).astype(F32)
@@ -315,11 +316,11 @@
         pltpu.roll(high, 32, 1),
         jnp.where(lane8 < 64, pltpu.roll(middle, 48, 1), pltpu.roll(rest - middle, 64, 1)),
     )
-    for n in range(NARROW):
-        rows = slice(YPART * n, YPART * (n + 1))
-        third_rows = jnp.where(lane8 < ZPART, last[rows], jnp.where(lane8 < 80, addends, 0.0))
-        piece = jnp.concatenate([first, spread[rows], third_rows], axis=0).astype(BF16)
-        whole_ref[:, n] = jnp.broadcast_to(piece[None], (WIDE, 24, 128))
+    addends = jnp.where((lane8 >= ZPART) & (lane8 < 80), addends, 0.0)
+    odd = lax.rem(w, 2) == 1
+    pair_ref[0:4] = top
+    pair_ref[4:8] = jnp.zeros((4, 128), F32)
+    pair_ref[8:16] = jnp.where(odd, pltpu.roll(addends, 48, 1), addends)
 
 
 def steps(w, recv, modes):
@@ -330,17 +331,48 @@
             pl.BlockSpec(memory_space=pltpu.VMEM),
             pl.BlockSpec(memory_space=pltpu.VMEM),
         ],
-        out_specs=pl.BlockSpec(memory_space=pltpu.VMEM),
-        out_shape=jax.ShapeDtypeStruct((WIDE, NARROW, 24, 128), BF16),
+        out_specs=[
+            pl.BlockSpec(memory_space=pltpu.VMEM),
+            pl.BlockSpec(memory_space=pltpu.VMEM),
+        ],
+        out_shape=[
+            jax.ShapeDtypeStruct((16, 128), F32),
+            jax.ShapeDtypeStruct((2, NY, 128), F32),
+        ],
         scratch_shapes=[
             pltpu.VMEM((3, 5, NY, 128), F32),
             pltpu.VMEM((3, 5, NY, 128), F32),
             pltpu.VMEM((3, 5, NY, 128), F32),
             pltpu.VMEM((5, 128, 128), F32),
+            pltpu.VMEM((2, 40, NY + 16, 128), F32),
         ],
         name="steps",
         compiler_params=pltpu.CompilerParams(vmem_limit_bytes=24 * 2**20),
     )(w, recv, modes)
+
+
+def merge_kernel(pair_ref, other_ref, home_ref, whole_ref):
+    both = pair_ref[...] + other_ref[...]
+    top = both[0:4]
+    high = top.astype(BF16).astype(F32)
+    first = jnp.concatenate([high, top - high], axis=0)
+    lane8 = lanes((8, 128))
+    for n in range(NARROW):
+        rows = slice(YPART * n, YPART * (n + 1))
+        third = jnp.where(lane8 < ZPART, home_ref[1, rows], both[8:16])
+        piece = jnp.concatenate([first, home_ref[0, rows], third], axis=0).astype(BF16)
+        whole_ref[:, n] = jnp.broadcast_to(piece[None], (CHIPS, 24, 128))
+
+
+def merge(pair, other, home):
+    return pl.pallas_call(
+        merge_kernel,
+        in_specs=[pl.BlockSpec(memory_space=pltpu.VMEM)] * 3,
+        out_specs=pl.BlockSpec(memory_space=pltpu.VMEM),
+        out_shape=jax.ShapeDtypeStruct((CHIPS, NARROW, 24, 128), BF16),
+        name="merge",
+        compiler_params=pltpu.CompilerParams(vmem_limit_bytes=16 * 2**20),
+    )(pair, other, home)
 
 
 def along_lanes(x, j):
@@ -389,16 +421,21 @@
     sums = jnp.sum(whole_ref[:, 0:8, :].astype(F32), axis=0)
     cross = sums[0:4] + sums[4:8]
     lane8 = lanes((8, 128))
-    source = lax.broadcasted_iota(jnp.int32, (COLS, 128), 0)
-    target = lanes((COLS, 128))
-    gram = jnp.zeros((COLS, 128), F32)
-    every = whole_ref[...].reshape(WIDE, NARROW, 24, 128)[:, :, 16:24, :].astype(F32)
+    source = lax.broadcasted_iota(jnp.int32, (COLS, 256), 0)
+    target = lanes((COLS, 256))
+    start = ZPART + 48 * (target // 128)
+    gram = jnp.zeros((CHIPS * 8, 256), F32)
+    every = whole_ref[...].reshape(CHIPS, NARROW, 24, 128)[:, :, 16:24, :].astype(F32)
     for b in range(8):
-        held = (source >= ZPART) & (source < ZPART + 48) & (target >= 16 * b)
-        chosen = jnp.where(held & (target == 16 * b + source % 16), 1.0, 0.0).astype(BF16)
-        rows = every[:, b].reshape(COLS, 128).astype(BF16)
+        held = (source >= start) & (source < start + 48)
+        match = target % 128 == 16 * b + source % 16
+        chosen = jnp.where(held & match, 1.0, 0.0).astype(BF16)
+        rows = every[:, b].reshape(CHIPS * 8, 128).astype(BF16)
         gram += jnp.dot(rows, chosen, preferred_element_type=F32)
-    panels = [gram[8 * a : 8 * a + 8] for a in range(16)]
+    panels = []
+    for a in range(16):
+        m, core = a // 2, a % 2
+        panels.append(gram[8 * m : 8 * m + 8, 128 * core : 128 * core + 128])
     panels[15] = jnp.concatenate([panels[15][0:4], cross], axis=0)
     turned = jnp.concatenate([panels[15]] * 16, axis=0).T
     for a in range(16):
@@ -406,7 +443,7 @@
     for a, rows in enumerate(factor_rows(panels)):
         factor_ref[8 * a : 8 * a + 8, :] = rows
 
-    home = whole_ref[pl.ds(w_ref[0] * NARROW, NARROW), 8:24, :].astype(F32)
+    home = whole_ref[pl.ds(lax.div(w_ref[0], 2) * NARROW, NARROW), 8:24, :].astype(F32)
     lane = lanes((YPART, 256))
     for c in range(5):
         total = jnp.zeros((YPART, 256), F32)
@@ -443,10 +480,18 @@
     modes = jnp.transpose(prior_modes[:, :, 0, :], (1, 0, 2))
     w = lax.axis_index("wide").astype(jnp.int32).reshape(1)
     sent, modes, known = pack(fields[:, 0], modes)
-    sent = sent.reshape(DEVICES, 16, 128)
+    sent, w = lax.optimization_barrier((sent.reshape(DEVICES, 16, 128), w))
     recv = lax.all_to_all(sent, EVERYWHERE, split_axis=0, concat_axis=0, tiled=True)
-    whole = steps(w, recv, modes).reshape(DEVICES, 24, 128)
-    whole = lax.all_to_all(whole, EVERYWHERE, split_axis=0, concat_axis=0, tiled=True)
+    pair, home = steps(w, recv, modes)
+    other = lax.ppermute(pair, "wide", [(i, i ^ 1) for i in range(WIDE)])
+    whole = merge(pair, other, home).reshape(CHIPS * NARROW, 24, 128)
+    groups = [
+        [(2 * m + core) * NARROW + n for m in range(CHIPS) for n in range(NARROW)]
+        for core in range(2)
+    ]
+    whole = lax.all_to_all(
+        whole, EVERYWHERE, split_axis=0, concat_axis=0, axis_index_groups=groups, tiled=True
+    )
     factor, state = finish(w, whole, known)
     return (state[:, None], factor)
 

time: 58.6 us -> 55.3 us (0.944)
  blocking collectives: 20.4 us -> 41.3 us
  waiting for transfers between devices: 13.4 us -> 1.16 us
  starting transfers between devices: 11.2 us -> 0.09 us
  Pallas kernels: 12.8 us -> 12 us
    all_to_all x1 -> x2, blocking collectives: 20.4 us -> 41.3 us  [the longest x1 24.3 us: local(): lax.all_to_all(sent, EVERYWHERE, split_axis=0, concat_axis=0, tiled=True)]
    all_to_all x1 -> x0, waiting for transfers between devices: 13.4 us -> none  [local(): lax.all_to_all(sent, EVERYWHERE, split_axis=0, concat_axis=0, tiled=True)]
    all_to_all x1 -> x0, starting transfers between devices: 11.2 us -> none  [local(): lax.all_to_all(sent, EVERYWHERE, split_axis=0, concat_axis=0, tiled=True)]
    ppermute x0 -> x1, waiting for transfers between devices: none -> 1.16 us  [local(): other = lax.ppermute(pair, 'wide', [(i, i ^ 1) for i in range(WIDE)])]
    pallas_call x1, Pallas kernels: 3.97 us -> 3.1 us  [pack(): pl.pallas_call(pack_kernel, in_specs=[pl.BlockSpec(memory_space=pltpu.HBM...]
where the time goes in v5:
time: 55.3 us; the launch traced here: 55.2 us
  blocking collectives  41.3 us (75%)
  Pallas kernels  12 us (22%)
  waiting for transfers between devices  1.16 us (2%)
  between operations  0.66 us (1%)
    all_to_all x1, blocking collectives, local(): lax.all_to_all(sent, EVERYWHERE, split_axis=0, concat_axis=0, tiled=True)  24.3 us
    all_to_all x1, blocking collectives, local(): lax.all_to_all(whole, EVERYWHERE, split_axis=0, concat_axis=0, axis_index...  16.9 us
    pallas_call x1, Pallas kernels, finish(): pl.pallas_call(finish_kernel, in_specs=[pl.BlockSpec(memory_space=pltpu.S...  5.01 us
    pallas_call x1, Pallas kernels, steps(): pl.pallas_call(step_kernel, in_specs=[pl.BlockSpec(memory_space=pltpu.SME...  3.82 us
    pallas_call x1, Pallas kernels, pack(): pl.pallas_call(pack_kernel, in_specs=[pl.BlockSpec(memory_space=pltpu.HBM...  3.1 us
    ppermute x1, waiting for transfers between devices, local(): other = lax.ppermute(pair, 'wide', [(i, i ^ 1) for i in range(WIDE)])  1.16 us
  transfers between devices with their start and end apart: 1, of which 1 were waited for; matrix products, arithmetic and copies ran while one was open for 0% of the time, Pallas kernels for 0%

profile of v5, /device:TPU:0, one launch (start us, length us, event | category | flops | bytes accessed | tf_op | source)
XLA Modules:
  0.0 55.2 jit_solution(14270883973911002161)
XLA Ops:
  0.6 3.1 %pack.1 = (bf16[16,8,16,128]{3,2,1,0:T(8,128)(2,1)S(1)}, bf16[5,124,2048]{2,1,0:T(8,128)(2,1)S(1)}, f32[5,8,256]{2,1,0:T(8,128)S(1)}) custom-call(f32[5,8,256]{2,1,0:T(8,128)} %bitcast.13, bf16[5,124,2048]{2,1,0:T(8,128)(2,1)} %bitcast.12), custom_call_target="tpu_custom_call" | custom-call | tf_op jit(solution)/shard_map/pack/pallas_call | solution.py:104
  3.7 24.3 %all_to_all.10.recv_ref = bf16[128,16,128]{2,1,0:T(8,128)(2,1)S(1)} all-to-all(bf16[128,16,128]{2,1,0:T(8,128)(2,1)S(1)} %bitcast.11), channel_id=1, replica_groups=mesh['wide'=16,'narrow'=8] {'wide','narrow'}, dimensions={0} | all-to-all | bytes 1048576 | tf_op jit(solution)/shard_map/all_to_all | solution.py:484
  28.1 3.8 %steps.1 = (f32[16,128]{1,0:T(8,128)S(1)}, f32[2,64,128]{2,1,0:T(8,128)S(1)}) custom-call(s32[1]{0:T(128)} %bitcast.4.w_ref, bf16[128,16,128]{2,1,0:T(8,128)(2,1)S(1)} %all_to_all.10.recv_ref, bf16[5,124,2048]{2,1,0:T(8,128)(2,1)S(1)} %get-tuple-element.14.modes_ref), custom_call_target="tpu_custom_call" | custom-call | tf_op jit(solution)/shard_map/steps/pallas_call | solution.py:327
  31.9 0.1 collective-permute-start
  32.0 1.2 %collective-permute-done.other_ref = f32[16,128]{1,0:T(8,128)S(1)} collective-permute-done((f32[16,128]{1,0:T(8,128)S(1)}, f32[16,128]{1,0:T(8,128)S(1)}, u32[]{:S(2)}, u32[]{:S(2)}) %collective-permute-start) | collective-permute-done | bytes 8224 | tf_op jit(solution)/shard_map/ppermute | solution.py:486
  33.2 16.9 %all_to_all.11.whole_ref = bf16[64,24,128]{2,1,0:T(8,128)(2,1)S(1)} all-to-all(bf16[64,24,128]{2,1,0:T(8,128)(2,1)S(1)} %bitcast.10), channel_id=1, replica_groups={{0,1,2,3,4,5,6,7,16,17,18,19,20,21,22,23,32,33,34,35,36,37,38,39,48,49,..., dimensions={0} | all-to-all | bytes 786432 | tf_op jit(solution)/shard_map/all_to_all | solution.py:492
  50.1 5.0 %finish.1 = (f32[128,128]{1,0:T(8,128)}, f32[5,8,256]{2,1,0:T(8,128)}) custom-call(s32[1]{0:T(128)} %bitcast.4.w_ref, bf16[64,24,128]{2,1,0:T(8,128)(2,1)S(1)} %all_to_all.11.whole_ref, f32[5,8,256]{2,1,0:T(8,128)S(1)} %get-tuple-element.17.known_ref), custom_call_target="tpu_custom_call" | custom-call | tf_op jit(solution)/shard_map/finish/pallas_call | solution.py:463
  (1 shorter events, 0.0 us)
Async XLA Ops:
  31.9 1.3 %collective-permute-start = (f32[16,128]{1,0:T(8,128)S(1)}, f32[16,128]{1,0:T(8,128)S(1)}, u32[]{:S(2)}, u32[]{:S(2)}) collective-permute-start(f32[16,128]{1,0:T(8,128)S(1)} %get-tuple-element.15.pair_ref), channel_id=1, source_target_pairs={{0,8},{8,0},{16,24},{24,16},{32,40},{40,32},{48,56},{56,48},{64,72... | collective-permute-start | bytes 24584 | tf_op jit(solution)/shard_map/ppermute | solution.py:486

commit v6 on v5

--- a/solution.py
+++ b/solution.py
@@ -293,18 +293,16 @@
     home_ref[0] = spread
     home_ref[1] = pltpu.roll(change[4], 128 - WINDOW - HALO, 1)
 
-    cross = jnp.zeros((4, MODES), F32)
-    square = jnp.zeros((4, 4), F32)
     contract = (((1,), (1,)), ((), ()))
     for c in range(5):
         rounded = packed[c].astype(BF16).astype(F32)
         pair = jnp.concatenate([rounded, pltpu.roll(rounded, 127, 1)], axis=0)
-        turn_ref[c] = pair.T
-    for c in range(5):
-        chunks = [turn_ref[c, pl.ds(2 * k, 4, stride=ZPART), :] for k in range(16)]
-        rows = jnp.concatenate(chunks, axis=1).astype(BF16)
-        cross += lax.dot_general(rows, modes_ref[c], contract, preferred_element_type=F32)
-        square += lax.dot_general(rows, rows, contract, preferred_element_type=F32)
+        turn_ref[c] = pair.astype(BF16).T.astype(F32)
+    chunks = [turn_ref[c, pl.ds(2 * k, 4, stride=ZPART), :] for c in range(5) for k in range(16)]
+    rows = jnp.concatenate(chunks, axis=1).astype(BF16)
+    every = jnp.concatenate([modes_ref[c] for c in range(5)], axis=1)
+    cross = lax.dot_general(rows, every, contract, preferred_element_type=F32)
+    square = lax.dot_general(rows, rows, contract, preferred_element_type=F32)
     top = jnp.concatenate([cross, square], axis=1) * INVERSE_CELLS
     lane8 = lanes((8, 128))
     block = block * INVERSE_CELLS
@@ -383,6 +381,19 @@
     return jnp.broadcast_to(x[i : i + 1, :], x.shape)
 
 
+NEAR = 2
+
+
+def tree(terms):
+    terms = list(terms)
+    while len(terms) > 1:
+        terms = [
+            terms[t] + terms[t + 1] if t + 1 < len(terms) else terms[t]
+            for t in range(0, len(terms), 2)
+        ]
+    return terms[0]
+
+
 def factor_rows(panels):
     panels = list(panels)
     lane = lanes((8, 128))
@@ -391,29 +402,49 @@
     done = []
     for k in range(count):
         base = 8 * k
-        later = range(k + 1, count)
+        near = range(k + 1, min(k + 1 + NEAR, count))
+        far = range(k + 1 + NEAR, count)
         columns = [along_lanes(panels[k], base + j) for j in range(8)]
         rows = [along_rows(panels[k], i) for i in range(8)]
-        below = {q: [along_lanes(panels[q], base + j) for j in range(8)] for q in later}
+        below = {q: [along_lanes(panels[q], base + j) for j in range(8)] for q in near}
         scaled = []
-        out = jnp.zeros((8, 128), F32)
+        unit = []
+        weights = {}
         for i in range(8):
             pivot = along_rows(columns[i], i)
             inverse = 1.0 / pivot
             for j in range(i + 1, 8):
                 weight = along_rows(columns[j], i) * inverse
+                weights[(i, j)] = weight
                 columns[j] = columns[j] - columns[i] * weight
                 rows[j] = rows[j] - rows[i] * weight
-                for q in later:
+                for q in near:
                     below[q][j] = below[q][j] - below[q][i] * weight
             scaled.append(rows[i] * inverse)
-            out = jnp.where(row == i, rows[i] * lax.rsqrt(pivot), out)
+            unit.append(rows[i] * lax.rsqrt(pivot))
+        out = unit[7]
+        for i in range(7):
+            out = jnp.where(row == i, unit[i], out)
         done.append(jnp.where(lane >= row + base, out, 0.0))
-        for q in later:
-            change = [below[q][i] * scaled[i] for i in range(8)]
-            while len(change) > 1:
-                change = [change[t] + change[t + 1] for t in range(0, len(change), 2)]
-            panels[q] = panels[q] - change[0]
+        for q in near:
+            panels[q] = panels[q] - tree(below[q][i] * scaled[i] for i in range(8))
+        if len(far):
+            answer = list(scaled)
+            for i in range(6, -1, -1):
+                answer[i] = scaled[i] - tree(
+                    [weights[(i, j)] * answer[j] for j in range(7, i, -1)]
+                )
+            solved = answer[7]
+            for i in range(7):
+                solved = jnp.where(row == i, answer[i], solved)
+            blank = jnp.zeros((8, 128), F32)
+            factor = jnp.concatenate([blank] * k + [solved] + [blank] * (15 - k), axis=0)
+            held = jnp.concatenate([panels[q] for q in far], axis=0)
+            change = jnp.dot(
+                held, factor, precision=lax.Precision.HIGHEST, preferred_element_type=F32
+            )
+            for t, q in enumerate(far):
+                panels[q] = panels[q] - change[8 * t : 8 * t + 8]
     return done
 
 

time: 55.3 us -> 54.6 us (0.987)
  Pallas kernels: 12 us -> 11.3 us
    pallas_call x1, Pallas kernels: 5.01 us -> 4.4 us  [finish(): pl.pallas_call(finish_kernel, in_specs=[pl.BlockSpec(memory_space=pltpu.S...]
where the time goes in v6:
time: 54.6 us; the launch traced here: 54.5 us
  blocking collectives  41.3 us (76%)
  Pallas kernels  11.3 us (21%)
  waiting for transfers between devices  1.16 us (2%)
  between operations  0.66 us (1%)
    all_to_all x1, blocking collectives, local(): lax.all_to_all(sent, EVERYWHERE, split_axis=0, concat_axis=0, tiled=True)  24.3 us
    all_to_all x1, blocking collectives, local(): lax.all_to_all(whole, EVERYWHERE, split_axis=0, concat_axis=0, axis_index...  16.9 us
    pallas_call x1, Pallas kernels, finish(): pl.pallas_call(finish_kernel, in_specs=[pl.BlockSpec(memory_space=pltpu.S...  4.4 us
    pallas_call x1, Pallas kernels, steps(): pl.pallas_call(step_kernel, in_specs=[pl.BlockSpec(memory_space=pltpu.SME...  3.74 us
    pallas_call x1, Pallas kernels, pack(): pl.pallas_call(pack_kernel, in_specs=[pl.BlockSpec(memory_space=pltpu.HBM...  3.1 us
    ppermute x1, waiting for transfers between devices, local(): other = lax.ppermute(pair, 'wide', [(i, i ^ 1) for i in range(WIDE)])  1.16 us
  transfers between devices with their start and end apart: 1, of which 1 were waited for; matrix products, arithmetic and copies ran while one was open for 0% of the time, Pallas kernels for 0%

profile of v6, /device:TPU:0, one launch (start us, length us, event | category | flops | bytes accessed | tf_op | source)
XLA Modules:
  0.0 54.5 jit_solution(10488533688134399800)
XLA Ops:
  0.6 3.1 %pack.1 = (bf16[16,8,16,128]{3,2,1,0:T(8,128)(2,1)S(1)}, bf16[5,124,2048]{2,1,0:T(8,128)(2,1)S(1)}, f32[5,8,256]{2,1,0:T(8,128)S(1)}) custom-call(f32[5,8,256]{2,1,0:T(8,128)} %bitcast.13, bf16[5,124,2048]{2,1,0:T(8,128)(2,1)} %bitcast.12), custom_call_target="tpu_custom_call" | custom-call | tf_op jit(solution)/shard_map/pack/pallas_call | solution.py:104
  3.7 24.3 %all_to_all.10.recv_ref = bf16[128,16,128]{2,1,0:T(8,128)(2,1)S(1)} all-to-all(bf16[128,16,128]{2,1,0:T(8,128)(2,1)S(1)} %bitcast.11), channel_id=1, replica_groups=mesh['wide'=16,'narrow'=8] {'wide','narrow'}, dimensions={0} | all-to-all | bytes 1048576 | tf_op jit(solution)/shard_map/all_to_all | solution.py:515
  28.1 3.7 %steps.1 = (f32[16,128]{1,0:T(8,128)S(1)}, f32[2,64,128]{2,1,0:T(8,128)S(1)}) custom-call(s32[1]{0:T(128)} %bitcast.4.w_ref, bf16[128,16,128]{2,1,0:T(8,128)(2,1)S(1)} %all_to_all.10.recv_ref, bf16[5,124,2048]{2,1,0:T(8,128)(2,1)S(1)} %get-tuple-element.14.modes_ref), custom_call_target="tpu_custom_call" | custom-call | tf_op jit(solution)/shard_map/steps/pallas_call | solution.py:325
  31.8 0.1 collective-permute-start
  31.9 1.2 %collective-permute-done.other_ref = f32[16,128]{1,0:T(8,128)S(1)} collective-permute-done((f32[16,128]{1,0:T(8,128)S(1)}, f32[16,128]{1,0:T(8,128)S(1)}, u32[]{:S(2)}, u32[]{:S(2)}) %collective-permute-start) | collective-permute-done | bytes 8224 | tf_op jit(solution)/shard_map/ppermute | solution.py:517
  33.1 16.9 %all_to_all.11.whole_ref = bf16[64,24,128]{2,1,0:T(8,128)(2,1)S(1)} all-to-all(bf16[64,24,128]{2,1,0:T(8,128)(2,1)S(1)} %bitcast.10), channel_id=1, replica_groups={{0,1,2,3,4,5,6,7,16,17,18,19,20,21,22,23,32,33,34,35,36,37,38,39,48,49,..., dimensions={0} | all-to-all | bytes 786432 | tf_op jit(solution)/shard_map/all_to_all | solution.py:523
  50.1 4.4 %finish.1 = (f32[128,128]{1,0:T(8,128)}, f32[5,8,256]{2,1,0:T(8,128)}) custom-call(s32[1]{0:T(128)} %bitcast.4.w_ref, bf16[64,24,128]{2,1,0:T(8,128)(2,1)S(1)} %all_to_all.11.whole_ref, f32[5,8,256]{2,1,0:T(8,128)S(1)} %get-tuple-element.17.known_ref), custom_call_target="tpu_custom_call" | custom-call | tf_op jit(solution)/shard_map/finish/pallas_call | solution.py:494
  (1 shorter events, 0.0 us)
Async XLA Ops:
  31.8 1.3 %collective-permute-start = (f32[16,128]{1,0:T(8,128)S(1)}, f32[16,128]{1,0:T(8,128)S(1)}, u32[]{:S(2)}, u32[]{:S(2)}) collective-permute-start(f32[16,128]{1,0:T(8,128)S(1)} %get-tuple-element.15.pair_ref), channel_id=1, source_target_pairs={{0,8},{8,0},{16,24},{24,16},{32,40},{40,32},{48,56},{56,48},{64,72... | collective-permute-start | bytes 24584 | tf_op jit(solution)/shard_map/ppermute | solution.py:517

commit v7 on v6

--- a/solution.py
+++ b/solution.py
@@ -269,13 +269,30 @@
             one[g, c] = v[c]
         if g == 1:
             keep(0, v, packed)
-    for g, v in section_all(stored(one), lane, edge, 3):
-        new = [0.5 * (base[g, c] + v[c]) for c in range(5)]
-        for c in range(5):
-            two[g, c] = new[c]
-        if g == 1:
-            keep(1, new, packed)
-    outer = [jnp.where(lane < WINDOW, two[2, c], two[0, c]) for c in range(5)]
+    first, middle, last = [stored(one)(g) for g in range(3)]
+    side = [jnp.where(lane < WINDOW, last[c], first[c]) for c in range(5)]
+    side_ahead, side_behind, side_total = within(side, edge, 3)
+    ahead, behind, total = within(middle, edge, 4)
+    far_ahead = across(last)[0]
+    v = joined(total, ahead, behind, side_ahead, side_behind, lane)
+    new = [0.5 * (base[1, c] + v[c]) for c in range(5)]
+    for c in range(5):
+        two[1, c] = new[c]
+    keep(1, new, packed)
+    outer = []
+    for c in range(5):
+        plus = jnp.where(
+            lane < WINDOW,
+            pltpu.roll(far_ahead[c], 128 - WINDOW, 1),
+            pltpu.roll(ahead[c], 2 * WINDOW, 1),
+        )
+        minus = jnp.where(
+            lane < WINDOW,
+            pltpu.roll(behind[c], 128 - 2 * WINDOW, 1),
+            pltpu.roll(side_behind[c], WINDOW, 1),
+        )
+        held = jnp.where(lane < WINDOW, base[2, c], base[0, c])
+        outer.append(0.5 * (held + (side_total[c] + (plus + minus))))
     after, before = across(outer)
     ahead, behind, total = within([two[1, c] for c in range(5)], edge, 6)
     third = joined(total, ahead, behind, after, before, lane)
@@ -340,7 +357,7 @@
         scratch_shapes=[
             pltpu.VMEM((3, 5, NY, 128), F32),
             pltpu.VMEM((3, 5, NY, 128), F32),
-            pltpu.VMEM((3, 5, NY, 128), F32),
+            pltpu.VMEM((2, 5, NY, 128), F32),
             pltpu.VMEM((5, 128, 128), F32),
             pltpu.VMEM((2, 40, NY + 16, 128), F32),
         ],

time: 54.6 us -> 54.5 us (level)
  no operation moved by 1% of the time
where the time goes in v7:
time: 54.5 us; the launch traced here: 54.3 us
  blocking collectives  41.3 us (76%)
  Pallas kernels  11.1 us (20%)
  waiting for transfers between devices  1.16 us (2%)
  between operations  0.66 us (1%)
    all_to_all x1, blocking collectives, local(): lax.all_to_all(sent, EVERYWHERE, split_axis=0, concat_axis=0, tiled=True)  24.3 us
    all_to_all x1, blocking collectives, local(): lax.all_to_all(whole, EVERYWHERE, split_axis=0, concat_axis=0, axis_index...  16.9 us
    pallas_call x1, Pallas kernels, finish(): pl.pallas_call(finish_kernel, in_specs=[pl.BlockSpec(memory_space=pltpu.S...  4.4 us
    pallas_call x1, Pallas kernels, steps(): pl.pallas_call(step_kernel, in_specs=[pl.BlockSpec(memory_space=pltpu.SME...  3.57 us
    pallas_call x1, Pallas kernels, pack(): pl.pallas_call(pack_kernel, in_specs=[pl.BlockSpec(memory_space=pltpu.HBM...  3.1 us
    ppermute x1, waiting for transfers between devices, local(): other = lax.ppermute(pair, 'wide', [(i, i ^ 1) for i in range(WIDE)])  1.16 us
  transfers between devices with their start and end apart: 1, of which 1 were waited for; matrix products, arithmetic and copies ran while one was open for 0% of the time, Pallas kernels for 0%

profile of v7, /device:TPU:0, one launch (start us, length us, event | category | flops | bytes accessed | tf_op | source)
XLA Modules:
  0.0 54.3 jit_solution(7733064190405323355)
XLA Ops:
  0.6 3.1 %pack.1 = (bf16[16,8,16,128]{3,2,1,0:T(8,128)(2,1)S(1)}, bf16[5,124,2048]{2,1,0:T(8,128)(2,1)S(1)}, f32[5,8,256]{2,1,0:T(8,128)S(1)}) custom-call(f32[5,8,256]{2,1,0:T(8,128)} %bitcast.13, bf16[5,124,2048]{2,1,0:T(8,128)(2,1)} %bitcast.12), custom_call_target="tpu_custom_call" | custom-call | tf_op jit(solution)/shard_map/pack/pallas_call | solution.py:104
  3.7 24.3 %all_to_all.10.recv_ref = bf16[128,16,128]{2,1,0:T(8,128)(2,1)S(1)} all-to-all(bf16[128,16,128]{2,1,0:T(8,128)(2,1)S(1)} %bitcast.11), channel_id=1, replica_groups=mesh['wide'=16,'narrow'=8] {'wide','narrow'}, dimensions={0} | all-to-all | bytes 1048576 | tf_op jit(solution)/shard_map/all_to_all | solution.py:532
  28.1 3.6 %steps.1 = (f32[16,128]{1,0:T(8,128)S(1)}, f32[2,64,128]{2,1,0:T(8,128)S(1)}) custom-call(s32[1]{0:T(128)} %bitcast.4.w_ref, bf16[128,16,128]{2,1,0:T(8,128)(2,1)S(1)} %all_to_all.10.recv_ref, bf16[5,124,2048]{2,1,0:T(8,128)(2,1)S(1)} %get-tuple-element.14.modes_ref), custom_call_target="tpu_custom_call" | custom-call | tf_op jit(solution)/shard_map/steps/pallas_call | solution.py:342
  31.7 0.1 collective-permute-start
  31.8 1.2 %collective-permute-done.other_ref = f32[16,128]{1,0:T(8,128)S(1)} collective-permute-done((f32[16,128]{1,0:T(8,128)S(1)}, f32[16,128]{1,0:T(8,128)S(1)}, u32[]{:S(2)}, u32[]{:S(2)}) %collective-permute-start) | collective-permute-done | bytes 8224 | tf_op jit(solution)/shard_map/ppermute | solution.py:534
  33.0 16.9 %all_to_all.11.whole_ref = bf16[64,24,128]{2,1,0:T(8,128)(2,1)S(1)} all-to-all(bf16[64,24,128]{2,1,0:T(8,128)(2,1)S(1)} %bitcast.10), channel_id=1, replica_groups={{0,1,2,3,4,5,6,7,16,17,18,19,20,21,22,23,32,33,34,35,36,37,38,39,48,49,..., dimensions={0} | all-to-all | bytes 786432 | tf_op jit(solution)/shard_map/all_to_all | solution.py:540
  49.9 4.4 %finish.1 = (f32[128,128]{1,0:T(8,128)}, f32[5,8,256]{2,1,0:T(8,128)}) custom-call(s32[1]{0:T(128)} %bitcast.4.w_ref, bf16[64,24,128]{2,1,0:T(8,128)(2,1)S(1)} %all_to_all.11.whole_ref, f32[5,8,256]{2,1,0:T(8,128)S(1)} %get-tuple-element.17.known_ref), custom_call_target="tpu_custom_call" | custom-call | tf_op jit(solution)/shard_map/finish/pallas_call | solution.py:511
  (1 shorter events, 0.0 us)
Async XLA Ops:
  31.7 1.3 %collective-permute-start = (f32[16,128]{1,0:T(8,128)S(1)}, f32[16,128]{1,0:T(8,128)S(1)}, u32[]{:S(2)}, u32[]{:S(2)}) collective-permute-start(f32[16,128]{1,0:T(8,128)S(1)} %get-tuple-element.15.pair_ref), channel_id=1, source_target_pairs={{0,8},{8,0},{16,24},{24,16},{32,40},{40,32},{48,56},{56,48},{64,72... | collective-permute-start | bytes 24584 | tf_op jit(solution)/shard_map/ppermute | solution.py:534

commit v8 on v7

--- a/solution.py
+++ b/solution.py
@@ -84,17 +84,16 @@
     rest = gram - high
     middle = rest.astype(BF16).astype(F32)
     low = rest - middle
+    group = lax.div(lane_full, 16)
+    middle_ahead = pltpu.roll(middle, 16, 1)
+    low_ahead = pltpu.roll(low, 32, 1)
     for n in range(NARROW):
-        def turned(x, place):
-            amount = (place - 16 * n) % 128
-            return pltpu.roll(x, amount, 1) if amount else x
-
         first, second = halves[n]
-        parts = jnp.where(
-            lane_full < 96,
-            turned(high, 80),
-            jnp.where(lane_full < 112, turned(middle, 96), turned(low, 112)),
-        ).reshape(WIDE, YPART, 128)
+        chosen = jnp.where(
+            group == n, high, jnp.where(group == (n + 1) % 8, middle_ahead, low_ahead)
+        )
+        amount = (80 - 16 * n) % 128
+        parts = (pltpu.roll(chosen, amount, 1) if amount else chosen).reshape(WIDE, YPART, 128)
         lower = jnp.broadcast_to(first[None], (WIDE, YPART, 128))
         upper = jnp.where(lane[None] < 2 * WINDOW, second[None], parts)
         out_ref[:, n] = jnp.concatenate([lower, upper], axis=1).astype(BF16)

time: 54.5 us -> 54.4 us (level)
  no operation moved by 1% of the time
where the time goes in v8:
time: 54.4 us; the launch traced here: 54.2 us
  blocking collectives  41.3 us (76%)
  Pallas kernels  11.1 us (20%)
  waiting for transfers between devices  1.16 us (2%)
  between operations  0.66 us (1%)
    all_to_all x1, blocking collectives, local(): lax.all_to_all(sent, EVERYWHERE, split_axis=0, concat_axis=0, tiled=True)  24.3 us
    all_to_all x1, blocking collectives, local(): lax.all_to_all(whole, EVERYWHERE, split_axis=0, concat_axis=0, axis_index...  16.9 us
    pallas_call x1, Pallas kernels, finish(): pl.pallas_call(finish_kernel, in_specs=[pl.BlockSpec(memory_space=pltpu.S...  4.4 us
    pallas_call x1, Pallas kernels, steps(): pl.pallas_call(step_kernel, in_specs=[pl.BlockSpec(memory_space=pltpu.SME...  3.57 us
    pallas_call x1, Pallas kernels, pack(): pl.pallas_call(pack_kernel, in_specs=[pl.BlockSpec(memory_space=pltpu.HBM...  3.05 us
    ppermute x1, waiting for transfers between devices, local(): other = lax.ppermute(pair, 'wide', [(i, i ^ 1) for i in range(WIDE)])  1.16 us
  transfers between devices with their start and end apart: 1, of which 1 were waited for; matrix products, arithmetic and copies ran while one was open for 0% of the time, Pallas kernels for 0%

profile of v8, /device:TPU:0, one launch (start us, length us, event | category | flops | bytes accessed | tf_op | source)
XLA Modules:
  0.0 54.2 jit_solution(15248027726857154100)
XLA Ops:
  0.6 3.0 %pack.1 = (bf16[16,8,16,128]{3,2,1,0:T(8,128)(2,1)S(1)}, bf16[5,124,2048]{2,1,0:T(8,128)(2,1)S(1)}, f32[5,8,256]{2,1,0:T(8,128)S(1)}) custom-call(f32[5,8,256]{2,1,0:T(8,128)} %bitcast.13, bf16[5,124,2048]{2,1,0:T(8,128)(2,1)} %bitcast.12), custom_call_target="tpu_custom_call" | custom-call | tf_op jit(solution)/shard_map/pack/pallas_call | solution.py:103
  3.7 24.3 %all_to_all.10.recv_ref = bf16[128,16,128]{2,1,0:T(8,128)(2,1)S(1)} all-to-all(bf16[128,16,128]{2,1,0:T(8,128)(2,1)S(1)} %bitcast.11), channel_id=1, replica_groups=mesh['wide'=16,'narrow'=8] {'wide','narrow'}, dimensions={0} | all-to-all | bytes 1048576 | tf_op jit(solution)/shard_map/all_to_all | solution.py:531
  28.0 3.6 %steps.1 = (f32[16,128]{1,0:T(8,128)S(1)}, f32[2,64,128]{2,1,0:T(8,128)S(1)}) custom-call(s32[1]{0:T(128)} %bitcast.4.w_ref, bf16[128,16,128]{2,1,0:T(8,128)(2,1)S(1)} %all_to_all.10.recv_ref, bf16[5,124,2048]{2,1,0:T(8,128)(2,1)S(1)} %get-tuple-element.14.modes_ref), custom_call_target="tpu_custom_call" | custom-call | tf_op jit(solution)/shard_map/steps/pallas_call | solution.py:341
  31.6 0.1 collective-permute-start
  31.7 1.2 %collective-permute-done.other_ref = f32[16,128]{1,0:T(8,128)S(1)} collective-permute-done((f32[16,128]{1,0:T(8,128)S(1)}, f32[16,128]{1,0:T(8,128)S(1)}, u32[]{:S(2)}, u32[]{:S(2)}) %collective-permute-start) | collective-permute-done | bytes 8224 | tf_op jit(solution)/shard_map/ppermute | solution.py:533
  32.9 16.9 %all_to_all.11.whole_ref = bf16[64,24,128]{2,1,0:T(8,128)(2,1)S(1)} all-to-all(bf16[64,24,128]{2,1,0:T(8,128)(2,1)S(1)} %bitcast.10), channel_id=1, replica_groups={{0,1,2,3,4,5,6,7,16,17,18,19,20,21,22,23,32,33,34,35,36,37,38,39,48,49,..., dimensions={0} | all-to-all | bytes 786432 | tf_op jit(solution)/shard_map/all_to_all | solution.py:539
  49.8 4.4 %finish.1 = (f32[128,128]{1,0:T(8,128)}, f32[5,8,256]{2,1,0:T(8,128)}) custom-call(s32[1]{0:T(128)} %bitcast.4.w_ref, bf16[64,24,128]{2,1,0:T(8,128)(2,1)S(1)} %all_to_all.11.whole_ref, f32[5,8,256]{2,1,0:T(8,128)S(1)} %get-tuple-element.17.known_ref), custom_call_target="tpu_custom_call" | custom-call | tf_op jit(solution)/shard_map/finish/pallas_call | solution.py:510
  (1 shorter events, 0.0 us)
Async XLA Ops:
  31.6 1.3 %collective-permute-start = (f32[16,128]{1,0:T(8,128)S(1)}, f32[16,128]{1,0:T(8,128)S(1)}, u32[]{:S(2)}, u32[]{:S(2)}) collective-permute-start(f32[16,128]{1,0:T(8,128)S(1)} %get-tuple-element.15.pair_ref), channel_id=1, source_target_pairs={{0,8},{8,0},{16,24},{24,16},{32,40},{40,32},{48,56},{56,48},{64,72... | collective-permute-start | bytes 24584 | tf_op jit(solution)/shard_map/ppermute | solution.py:533
